TPU v7x, 512 devices: a whole 4x8x8 slice. The times are simulated.
512 devices in a mesh: slab: 16 (over z, core), dom: 32 (over x, y).
Axes of the slice: x: 4, y: 8, z: 8, core: 2. Of those that a mesh axis runs over, the one named last changes fastest.
Arguments:
- positions: float32 [3, 262144], P(None, ('slab', 'dom')), may hold values from -0.5 to 64.5, as said below
- burgers: float32 [3, 262144], P(None, ('slab', 'dom')), may hold values from -6 to 6
- mobility: float32 [262144], P(('slab', 'dom')), may hold values from 0.5 to 2
- block_cells: int32 [2048], P(('slab', 'dom')), may hold values from 0 to 255, as said below
- pairs: int32 [32768, 2], P(('slab', 'dom')), may hold values from 0 to 2047, as said below
- pair_count: int32 [512], P(('slab', 'dom')), may hold values from 8 to 64, as said below
Outputs:
- moved: float32 [3, 262144], P(None, ('slab', 'dom'))
- velocity: float32 [3, 262144], P(None, ('slab', 'dom'))
Inputs may be any that keep to these rules, and one draw needn't show every extreme that they name: `block_cells`: block k lies in slab k // (4 * 32) and its cell is 16 times that slab plus 0 to 15. `positions`: each segment lies within 2.5 of its block's cell centre along x and within 1.5 along y and z. `pairs`: device d = s * 32 + e owns blocks d * 4 to (d + 1) * 4 - 1. In device d's slots the first block is one of its own; the second is owned by a device of slab s - 1, s or s + 1 at dom position e - 1, e or e + 1, and differs from the first. Every slot holds such a pair, used or not. `pair_count`: in each slab exactly one device has 64 used slots; the others have at most 32.
All inputs are finite; a program needn't handle non-finite values.
Results may differ from a plain program's by a relative error of at most 0.0003.
Values sent between devices are 32-bit elements; how exact they have to be, the bound alone decides.
A program may use at most 64 MiB of HBM per device.

v0:
```python
import math

import jax
import jax.numpy as jnp
from jax import lax
from jax.sharding import PartitionSpec as P

BLOCK_SEGS = 128


core_near = 0.25
core_far = 9.0
time_increment = 0.25
pair_batch = 4
hi_prec = lax.Precision.HIGHEST


def padded(x, sides, width):
    for axis, dim in sides:
        peers, length = (lax.axis_size(axis), x.shape[dim])
        up = [(i, (i + 1) % peers) for i in range(peers - 1)]
        down = [(j, i) for i, j in up]
        last = lax.slice_in_dim(x, length - width, length, axis=dim)
        initial = lax.slice_in_dim(x, 0, width, axis=dim)
        before = lax.ppermute(last, axis, up)
        after = lax.ppermute(initial, axis, down)
        x = jnp.concatenate([before, x, after], axis=dim)
    return x


def shifted(block, axis, distance):
    devices = range(lax.axis_size(axis))
    route = [(i - distance, i) for i in devices if i - distance in devices]
    return lax.ppermute(block, axis, route)


def from_everyone(x, axis):
    peers = lax.axis_size(axis)
    return lax.all_to_all(jnp.broadcast_to(x[None], (peers, *x.shape)), axis, 0, 0, tiled=True)


def of_everyone(x, axis):
    everything = from_everyone(x, axis)
    return jnp.sum(everything, axis=0)


def laid_out(pieces, dim):
    lengths = list(pieces.shape[1:])
    lengths[dim] *= pieces.shape[0]
    return jnp.moveaxis(pieces, 0, dim).reshape(lengths)


def gathered_copies(x, axis, dim):
    pieces = from_everyone(x, axis)
    return laid_out(pieces, dim)


def centers(cells):
    slabs = cells // 16
    rest = cells % 16
    return jnp.stack([4 * slabs + 2, 2 * (rest // 4) + 1, 2 * (rest % 4) + 1]).astype(jnp.float32)


def block_moments(posit, burg, cells, ncells, width, base_cell):
    nblk = cells.shape[0]
    offset = posit.reshape(3, nblk, width) - centers(cells)[:, :, None]
    vec = burg.reshape(3, nblk, width)
    first = (vec[:, None] * offset[None]).reshape(9, nblk, width)
    second = (vec[:, None, None] * offset[None, :, None] * offset[None, None, :]).reshape(
        27, nblk, width
    )
    rows = jnp.sum(jnp.concatenate([vec, first, second], axis=0), axis=2)
    onehot = ((cells - base_cell)[:, None] == jnp.arange(ncells, dtype=jnp.int32)[None, :]).astype(
        jnp.float32
    )
    return jnp.dot(rows, onehot, precision=hi_prec)


def far_field(posit, burg, moments):
    ncells = moments.shape[1]
    nblk = ncells // 64
    zeds = centers(jnp.arange(ncells, dtype=jnp.int32)).reshape(3, nblk, 64).transpose(1, 0, 2)
    mblk = moments.reshape(39, nblk, 64).transpose(1, 0, 2)

    def visit(acc, item):
        zpart, mpart = item
        r = posit[:, None, :] - zpart[:, :, None]
        sq = r[0] * r[0] + r[1] * r[1] + r[2] * r[2] + core_far
        inv3 = 1.0 / (sq * jnp.sqrt(sq))
        inv5 = inv3 / sq
        inv7 = inv5 / sq
        qzero = jnp.einsum("kc,kn->cn", mpart[0:3], burg, precision=hi_prec)
        qone = jnp.einsum("kac,kn->acn", mpart[3:12].reshape(3, 3, 64), burg, precision=hi_prec)
        qtwo = jnp.einsum(
            "kabc,kn->abcn", mpart[12:39].reshape(3, 3, 3, 64), burg, precision=hi_prec
        )
        qone_r = jnp.sum(qone * r, axis=0)
        qtwo_r = jnp.sum(qtwo * r[None], axis=1)
        rqr = jnp.sum(r * qtwo_r, axis=0)
        trace = qtwo[0, 0] + qtwo[1, 1] + qtwo[2, 2]
        scal = qzero * inv3 + 3.0 * qone_r * inv5 - 1.5 * trace * inv5 + 7.5 * rqr * inv7
        force = r * scal[None] - qone * inv3[None] - 3.0 * qtwo_r * inv5[None]
        return (acc + jnp.sum(force, axis=1), None)

    start = jnp.zeros(posit.shape, jnp.float32)
    total, unused = lax.scan(visit, start, (zeds, mblk))
    return total


def pair_forces(pos_a, bur_a, pos_b, bur_b, weight):
    r = pos_a[:, :, :, None] - pos_b[:, :, None, :]
    sq = r[0] * r[0] + r[1] * r[1] + r[2] * r[2]
    near_s = sq + core_near
    far_s = sq + core_far
    kern = 1.0 / (near_s * jnp.sqrt(near_s)) - 1.0 / (far_s * jnp.sqrt(far_s))
    coef = jnp.sum(bur_a[:, :, :, None] * bur_b[:, :, None, :], axis=0)
    wgt = weight[:, None, None] * coef * kern
    wr = wgt[None] * r
    return (jnp.sum(wr, axis=3), -jnp.sum(wr, axis=2))


def around_all(stacked):
    grown = padded(stacked[:, None, None, :], (("slab", 1), ("dom", 2)), 1)
    return grown.reshape(stacked.shape[0], -1)


def around_moved(posit):
    grown = padded(posit[:, None, None, :], (("slab", 1), ("dom", 2)), 1)
    return grown.reshape(posit.shape[0], -1)


def give_around(window_force, per_dev):
    grid = window_force.reshape(3, 3, 3, per_dev)
    from_above = shifted(grid[:, 0], "slab", -1)
    from_below = shifted(grid[:, 2], "slab", 1)
    row = grid[:, 1] + from_above + from_below
    from_right = shifted(row[:, 0], "dom", -1)
    from_left = shifted(row[:, 2], "dom", 1)
    return row[:, 1] + from_right + from_left


def body(positions, burgers, mobility, block_cells, pairs, pair_count):
    count_segs = positions.shape[1]
    width = BLOCK_SEGS
    n_slab = lax.axis_size("slab")
    n_dom = lax.axis_size("dom")
    ncells = 16 * n_slab
    blk_dev = block_cells.shape[0]
    far_scale = math.sqrt(ncells / (count_segs * n_slab * n_dom))
    slots = pairs.shape[0]
    my_slab = lax.axis_index("slab")
    my_dom = lax.axis_index("dom")
    used = pair_count[0]

    def locate(rotation_slots):
        return pairs[jnp.minimum(rotation_slots, slots - 1)]

    def to_window(blocks):
        owner = blocks // blk_dev
        within = blocks % blk_dev
        row_off = owner // n_dom - my_slab + 1
        col_off = owner % n_dom - my_dom + 1
        return jnp.clip((row_off * 3 + col_off) * blk_dev + within, 0, 9 * blk_dev - 1)

    def near(window):
        pos_win = window[0:3].reshape(3, -1, width)
        bur_win = window[3:6].reshape(3, -1, width)

        def turn(index, acc):
            rotation_slots = index * pair_batch + jnp.arange(pair_batch, dtype=jnp.int32)
            weight = (rotation_slots < used).astype(jnp.float32)
            chosen = locate(rotation_slots)
            first_blk = to_window(chosen[:, 0])
            second_blk = to_window(chosen[:, 1])
            force_a, force_b = pair_forces(
                pos_win[:, first_blk],
                bur_win[:, first_blk],
                pos_win[:, second_blk],
                bur_win[:, second_blk],
                weight,
            )
            return acc.at[:, first_blk].add(force_a).at[:, second_blk].add(force_b)

        groups = (used + pair_batch - 1) // pair_batch
        start = jnp.zeros(pos_win.shape, jnp.float32)
        return lax.fori_loop(0, groups, turn, start).reshape(3, -1)

    def gather_moments(posit):
        local = block_moments(posit, burgers, block_cells, 16, width, 16 * my_slab)
        summed = of_everyone(local, "dom")
        return gathered_copies(summed, "slab", 1)

    def speed(posit, window):
        moments = gather_moments(posit)
        far = far_field(posit, burgers, moments)
        near_own = give_around(near(window), count_segs)
        return mobility[None, :] * (far_scale * far + near_own)

    stacked = jnp.concatenate([positions, burgers], axis=0)
    leading_window = around_all(stacked)
    first_v = speed(positions, leading_window)
    stepped = positions + time_increment * first_v
    moved_win = around_moved(stepped)
    window_second = jnp.concatenate([moved_win, leading_window[3:6]], axis=0)
    second_v = speed(stepped, window_second)
    total = first_v + second_v
    return (positions + 0.5 * time_increment * total, 0.5 * total)


def solution(mesh):
    placed = (
        P(None, ("slab", "dom")),
        P(None, ("slab", "dom")),
        P(("slab", "dom")),
        P(("slab", "dom")),
        P(("slab", "dom"), None),
        P(("slab", "dom")),
    )
    return jax.shard_map(
        body,
        mesh=mesh,
        in_specs=placed,
        out_specs=(P(None, ("slab", "dom")), P(None, ("slab", "dom"))),
        check_vma=False,
    )
```

profile of v0, /device:TPU:1, one launch (start us, length us, event | category | flops | bytes accessed | tf_op | source)
XLA Modules:
  0.0 348.7 jit_solution(688982446653196454)
XLA Ops:
  0.6 0.7 maximum_bitcast_fusion
  1.4 8.7 %collective-permute-start.1 = (f32[6,1,1,512]{3,0,2,1:T(8,128)S(1)}, f32[6,1,1,512]{3,0,2,1:T(8,128)S(1)}, u32[]{:S(2)}, u32[]{:S(2)}) collective-permute-start(f32[6,1,1,512]{3,0,2,1:T(8,128)S(1)} %maximum_bitcast_fusion), channel_id=1, source_target_pairs={{32,0},{64,32},{96,64},{128,96},{160,128},{192,160},{224,192},{256... | collective-permute-start | bytes 36872 | tf_op jit(solution)/shard_map/ppermute | solution.py:26
  10.1 1.9 collective-permute-start
  12.0 0.7 reshape.398
  12.8 0.7 reshape.399
  13.5 0.7 add_bitcast_fusion.1
  14.7 0.9 reshape.529
  15.6 6.3 %all-to-all-start = ((f32[32,1,624]{2,1,0:T(1,128)}), f32[32,1,624]{2,1,0:T(1,128)S(1)}, u32[]{:S(2)}, u32[]{:S(2)}) async-start(f32[32,1,624]{2,1,0:T(1,128)} %reshape.529), calls=%async_computation | async-start | bytes 163840 | tf_op jit(solution)/shard_map/all_to_all | solution.py:39
  21.9 1.3 collective-permute-start.3
  23.2 4.0 %collective-permute-start.2 = (f32[6,3,1,512]{3,0,2,1:T(8,128)S(1)}, f32[6,3,1,512]{3,0,2,1:T(8,128)S(1)}, u32[]{:S(2)}, u32[]{:S(2)}) collective-permute-start(f32[6,3,1,512]{3,0,2,1:T(8,128)S(1)} %pad_maximum_fusion.4), channel_id=1, source_target_pairs={{0,1},{1,2},{2,3},{3,4},{4,5},{5,6},{6,7},{7,8},{8,9},{9,10},{10,1... | collective-permute-start | bytes 110600 | tf_op jit(solution)/shard_map/ppermute | solution.py:25
  28.5 32.9 %while.48 = (s32[]{:T(128)}, f32[3,36,128]{2,0,1:T(4,128)S(1)}, s32[]{:T(128)}, s32[64,2]{1,0:T(8,128)S(1)}, s32[]{:T(128)}, /*index=5*/s32[]{:T(128)}, s32[]{:T...) while((s32[]{:T(128)}, f32[3,36,128]{2,0,1:T(4,128)S(1)}, ...), condition=%wide.region_14.15_spmd, body=%wide.region_8.14_spmd.sunk | while | flops 2233267 | bytes 2855389 | solution.py:186
  28.5 0.7 compare_convert_fusion.4
  33.7 0.6 scatter_fusion
  35.1 0.7 compare_convert_fusion.4
  40.3 0.6 scatter_fusion
  41.6 0.7 compare_convert_fusion.4
  46.9 0.6 scatter_fusion
  48.2 0.7 compare_convert_fusion.4
  53.5 0.6 scatter_fusion
  54.8 0.7 compare_convert_fusion.4
  61.4 1.9 collective-permute-start.4
  63.3 3.6 %collective-permute-start.5 = (f32[3,3,512]{2,0,1:T(4,128)S(1)}, f32[3,3,512]{2,0,1:T(4,128)S(1)}, u32[]{:S(2)}, u32[]{:S(2)}) collective-permute-start(f32[3,3,512]{2,0,1:T(4,128)S(1)} %get-tuple-element.641), channel_id=1, source_target_pairs={{0,32},{32,64},{64,96},{96,128},{128,160},{160,192},{192,224},{224... | collective-permute-start | bytes 55304 | tf_op jit(solution)/shard_map/ppermute | solution.py:34
  67.0 0.9 collective-permute-done.5
  68.5 0.8 reduce.12
  69.5 0.8 reshape.531
  70.2 28.6 %all-to-all-start.1 = ((f32[16,1,624]{2,1,0:T(1,128)}), f32[16,1,624]{2,1,0:T(1,128)S(1)}, u32[]{:S(2)}, u32[]{:S(2)}) async-start(f32[16,1,624]{2,1,0:T(1,128)} %reshape.531), calls=%async_computation.1 | async-start | bytes 81920 | tf_op jit(solution)/shard_map/all_to_all | solution.py:39
  98.8 1.3 collective-permute-start.6
  100.1 6.5 %collective-permute-start.7 = (f32[3,512]{1,0:T(4,128)S(1)}, f32[3,512]{1,0:T(4,128)S(1)}, u32[]{:S(2)}, u32[]{:S(2)}) collective-permute-start(f32[3,512]{1,0:T(4,128)S(1)} %get-tuple-element.645), channel_id=1, source_target_pairs={{0,1},{1,2},{2,3},{3,4},{4,5},{5,6},{6,7},{7,8},{8,9},{9,10},{10,1... | collective-permute-start | bytes 18440 | tf_op jit(solution)/shard_map/ppermute | solution.py:34
  106.6 0.7 reduce.13
  107.5 10.6 %while.50 = (s32[]{:T(128)}, f32[3,512]{1,0:T(4,128)S(1)}, f32[3,512]{1,0:T(4,128)S(1)}, f32[4,3,64]{2,1,0:T(4,128)S(1)}, f32[4,39,64]{2,1,0:T(8,128)S(1)}, /*in...) while((s32[]{:T(128)}, f32[3,512]{1,0:T(4,128)S(1)}, f32[3,512]{1,0:T(4,128)S(1)}, ...), condition=%wide.region_7.8_spmd.clone, body=%wide.region_2.7_spmd.clone.sunk | while | flops 18023940 | bytes 6538151 | solution.py:106
  107.9 1.2 multiply_reduce_fusion.18
  110.5 1.2 multiply_reduce_fusion.18
  113.2 1.2 multiply_reduce_fusion.18
  115.8 1.2 multiply_reduce_fusion.18
  118.2 2.3 collective-permute-start.9
  120.5 3.5 collective-permute-start.8
  124.8 1.3 collective-permute-start.11
  126.0 5.9 %collective-permute-start.10 = (f32[3,3,1,512]{3,0,2,1:T(4,128)S(1)}, f32[3,3,1,512]{3,0,2,1:T(4,128)S(1)}, u32[]{:S(2)}, u32[]{:S(2)}) collective-permute-start(f32[3,3,1,512]{3,0,2,1:T(4,128)S(1)} %pad_maximum_fusion.5), channel_id=1, source_target_pairs={{0,1},{1,2},{2,3},{3,4},{4,5},{5,6},{6,7},{7,8},{8,9},{9,10},{10,1... | collective-permute-start | bytes 55304 | tf_op jit(solution)/shard_map/ppermute | solution.py:25
  132.2 0.7 collective-permute-done.10
  132.9 32.9 %while.49 = (s32[]{:T(128)}, f32[3,36,128]{2,0,1:T(4,128)S(1)}, s32[]{:T(128)}, s32[64,2]{1,0:T(8,128)S(1)}, s32[]{:T(128)}, /*index=5*/s32[]{:T(128)}, s32[]{:T...) while((s32[]{:T(128)}, f32[3,36,128]{2,0,1:T(4,128)S(1)}, ...), condition=%wide.region_29.30_spmd, body=%wide.region_23.29_spmd.sunk | while | flops 2233267 | bytes 2855389 | solution.py:186
  133.0 0.7 compare_convert_fusion.5
  138.2 0.6 scatter_fusion.2
  139.5 0.7 compare_convert_fusion.5
  144.8 0.6 scatter_fusion.2
  146.1 0.7 compare_convert_fusion.5
  152.7 0.7 compare_convert_fusion.5
  159.3 0.7 compare_convert_fusion.5
  165.9 1.9 collective-permute-start.12
  167.8 3.6 %collective-permute-start.13 = (f32[3,3,512]{2,0,1:T(4,128)S(1)}, f32[3,3,512]{2,0,1:T(4,128)S(1)}, u32[]{:S(2)}, u32[]{:S(2)}) collective-permute-start(f32[3,3,512]{2,0,1:T(4,128)S(1)} %get-tuple-element.639), channel_id=1, source_target_pairs={{0,32},{32,64},{64,96},{96,128},{128,160},{160,192},{192,224},{224... | collective-permute-start | bytes 55304 | tf_op jit(solution)/shard_map/ppermute | solution.py:34
  171.5 0.9 reshape.533
  172.3 136.1 %all-to-all-start.2 = ((f32[32,1,624]{2,1,0:T(1,128)}), f32[32,1,624]{2,1,0:T(1,128)S(1)}, u32[]{:S(2)}, u32[]{:S(2)}) async-start(f32[32,1,624]{2,1,0:T(1,128)} %reshape.533), calls=%async_computation.2 | async-start | bytes 163840 | tf_op jit(solution)/shard_map/all_to_all | solution.py:39
  308.5 9.0 %all-to-all-done.2 = f32[32,1,624]{2,1,0:T(1,128)S(1)} async-done(((f32[32,1,624]{2,1,0:T(1,128)}), f32[32,1,624]{2,1,0:T(1,128)S(1)}, u32[]{:S(2)}, u32[]{:S(2)}) %all-to-all-start.2) | async-done | bytes 79904 | tf_op jit(solution)/shard_map/all_to_all | solution.py:39
  317.5 0.8 reduce.14
  318.5 0.8 reshape.535
  319.3 9.2 %all-to-all-start.3 = ((f32[16,1,624]{2,1,0:T(1,128)}), f32[16,1,624]{2,1,0:T(1,128)S(1)}, u32[]{:S(2)}, u32[]{:S(2)}) async-start(f32[16,1,624]{2,1,0:T(1,128)} %reshape.535), calls=%async_computation.3 | async-start | bytes 81920 | tf_op jit(solution)/shard_map/all_to_all | solution.py:39
  328.5 1.3 collective-permute-start.14
  329.8 4.0 %collective-permute-start.15 = (f32[3,512]{1,0:T(4,128)S(1)}, f32[3,512]{1,0:T(4,128)S(1)}, u32[]{:S(2)}, u32[]{:S(2)}) collective-permute-start(f32[3,512]{1,0:T(4,128)S(1)} %get-tuple-element.643), channel_id=1, source_target_pairs={{0,1},{1,2},{2,3},{3,4},{4,5},{5,6},{6,7},{7,8},{8,9},{9,10},{10,1... | collective-permute-start | bytes 18440 | tf_op jit(solution)/shard_map/ppermute | solution.py:34
  333.8 2.1 all-to-all-done.3
  335.9 0.7 reduce.15
  336.8 10.6 %while.51 = (s32[]{:T(128)}, f32[3,512]{1,0:T(4,128)S(1)}, f32[3,512]{1,0:T(4,128)S(1)}, f32[4,3,64]{2,1,0:T(4,128)S(1)}, f32[4,39,64]{2,1,0:T(8,128)S(1)}, /*in...) while((s32[]{:T(128)}, f32[3,512]{1,0:T(4,128)S(1)}, f32[3,512]{1,0:T(4,128)S(1)}, ...), condition=%wide.region_22.23_spmd.clone, body=%wide.region_17.22_spmd.clone.sunk | while | flops 18023940 | bytes 6538151 | solution.py:106
  337.2 1.2 multiply_reduce_fusion.19
  339.8 1.2 multiply_reduce_fusion.19
  342.5 1.2 multiply_reduce_fusion.19
  345.1 1.2 multiply_reduce_fusion.19
  (383 shorter events, 70.4 us)
Async XLA Ops:
  0.6 27.3 %copy-start.3 = (s32[64,2]{0,1:T(2,128)S(1)}, s32[64,2]{0,1:T(2,128)}, u32[]{:S(2)}) copy-start(s32[64,2]{0,1:T(2,128)} %param.18) | copy-start | bytes 1540
  1.4 20.5 %collective-permute-start.1 = (f32[6,1,1,512]{3,0,2,1:T(8,128)S(1)}, f32[6,1,1,512]{3,0,2,1:T(8,128)S(1)}, u32[]{:S(2)}, u32[]{:S(2)}) collective-permute-start(f32[6,1,1,512]{3,0,2,1:T(8,128)S(1)} %maximum_bitcast_fusion), channel_id=1, source_target_pairs={{32,0},{64,32},{96,64},{128,96},{160,128},{192,160},{224,192},{256... | collective-permute-start | bytes 36872 | tf_op jit(solution)/shard_map/ppermute | solution.py:26
  10.1 11.8 %collective-permute-start = (f32[6,1,1,512]{3,0,2,1:T(8,128)S(1)}, f32[6,1,1,512]{3,0,2,1:T(8,128)S(1)}, u32[]{:S(2)}, u32[]{:S(2)}) collective-permute-start(f32[6,1,1,512]{3,0,2,1:T(8,128)S(1)} %maximum_bitcast_fusion), channel_id=1, source_target_pairs={{0,32},{32,64},{64,96},{96,128},{128,160},{160,192},{192,224},{224... | collective-permute-start | bytes 36872 | tf_op jit(solution)/shard_map/ppermute | solution.py:25
  15.6 52.4 %all-to-all-start = ((f32[32,1,624]{2,1,0:T(1,128)}), f32[32,1,624]{2,1,0:T(1,128)S(1)}, u32[]{:S(2)}, u32[]{:S(2)}) async-start(f32[32,1,624]{2,1,0:T(1,128)} %reshape.529), calls=%async_computation | async-start | bytes 163840 | tf_op jit(solution)/shard_map/all_to_all | solution.py:39
  21.9 6.1 %collective-permute-start.3 = (f32[6,3,1,512]{3,0,2,1:T(8,128)S(1)}, f32[6,3,1,512]{3,0,2,1:T(8,128)S(1)}, u32[]{:S(2)}, u32[]{:S(2)}) collective-permute-start(f32[6,3,1,512]{3,0,2,1:T(8,128)S(1)} %pad_maximum_fusion.4), channel_id=1, source_target_pairs={{1,0},{2,1},{3,2},{4,3},{5,4},{6,5},{7,6},{8,7},{9,8},{10,9},{11,1... | collective-permute-start | bytes 110600 | tf_op jit(solution)/shard_map/ppermute | solution.py:26
  23.2 5.2 %collective-permute-start.2 = (f32[6,3,1,512]{3,0,2,1:T(8,128)S(1)}, f32[6,3,1,512]{3,0,2,1:T(8,128)S(1)}, u32[]{:S(2)}, u32[]{:S(2)}) collective-permute-start(f32[6,3,1,512]{3,0,2,1:T(8,128)S(1)} %pad_maximum_fusion.4), channel_id=1, source_target_pairs={{0,1},{1,2},{2,3},{3,4},{4,5},{5,6},{6,7},{7,8},{8,9},{9,10},{10,1... | collective-permute-start | bytes 110600 | tf_op jit(solution)/shard_map/ppermute | solution.py:25
  61.4 46.1 %copy-start = (f32[3,512]{1,0:T(4,128)S(1)}, f32[3,512]{1,0:T(4,128)}, u32[]{:S(2)}) copy-start(f32[3,512]{1,0:T(4,128)} %param.15) | copy-start | bytes 18436
  61.4 46.1 %copy-start.1 = (f32[3,512]{1,0:T(4,128)S(1)}, f32[3,512]{1,0:T(4,128)}, u32[]{:S(2)}) copy-start(f32[3,512]{1,0:T(4,128)} %param.14) | copy-start | bytes 18436
  61.4 5.6 %collective-permute-start.4 = (f32[3,3,512]{2,0,1:T(4,128)S(1)}, f32[3,3,512]{2,0,1:T(4,128)S(1)}, u32[]{:S(2)}, u32[]{:S(2)}) collective-permute-start(f32[3,3,512]{2,0,1:T(4,128)S(1)} %get-tuple-element.640), channel_id=1, source_target_pairs={{32,0},{64,32},{96,64},{128,96},{160,128},{192,160},{224,192},{256... | collective-permute-start | bytes 55304 | tf_op jit(solution)/shard_map/ppermute | solution.py:34
  63.3 4.6 %collective-permute-start.5 = (f32[3,3,512]{2,0,1:T(4,128)S(1)}, f32[3,3,512]{2,0,1:T(4,128)S(1)}, u32[]{:S(2)}, u32[]{:S(2)}) collective-permute-start(f32[3,3,512]{2,0,1:T(4,128)S(1)} %get-tuple-element.641), channel_id=1, source_target_pairs={{0,32},{32,64},{64,96},{96,128},{128,160},{160,192},{192,224},{224... | collective-permute-start | bytes 55304 | tf_op jit(solution)/shard_map/ppermute | solution.py:34
  70.2 36.4 %all-to-all-start.1 = ((f32[16,1,624]{2,1,0:T(1,128)}), f32[16,1,624]{2,1,0:T(1,128)S(1)}, u32[]{:S(2)}, u32[]{:S(2)}) async-start(f32[16,1,624]{2,1,0:T(1,128)} %reshape.531), calls=%async_computation.1 | async-start | bytes 81920 | tf_op jit(solution)/shard_map/all_to_all | solution.py:39
  98.8 19.4 %collective-permute-start.6 = (f32[3,512]{1,0:T(4,128)S(1)}, f32[3,512]{1,0:T(4,128)S(1)}, u32[]{:S(2)}, u32[]{:S(2)}) collective-permute-start(f32[3,512]{1,0:T(4,128)S(1)} %get-tuple-element.644), channel_id=1, source_target_pairs={{1,0},{2,1},{3,2},{4,3},{5,4},{6,5},{7,6},{8,7},{9,8},{10,9},{11,1... | collective-permute-start | bytes 18440 | tf_op jit(solution)/shard_map/ppermute | solution.py:34
  100.1 18.1 %collective-permute-start.7 = (f32[3,512]{1,0:T(4,128)S(1)}, f32[3,512]{1,0:T(4,128)S(1)}, u32[]{:S(2)}, u32[]{:S(2)}) collective-permute-start(f32[3,512]{1,0:T(4,128)S(1)} %get-tuple-element.645), channel_id=1, source_target_pairs={{0,1},{1,2},{2,3},{3,4},{4,5},{5,6},{6,7},{7,8},{8,9},{9,10},{10,1... | collective-permute-start | bytes 18440 | tf_op jit(solution)/shard_map/ppermute | solution.py:34
  107.5 10.7 %copy-start.2 = (f32[512]{0:T(512)S(1)}, f32[512]{0:T(512)}, u32[]{:S(2)}) copy-start(f32[512]{0:T(512)} %param.16) | copy-start | bytes 6148
  118.2 6.0 %collective-permute-start.9 = (f32[3,1,1,512]{3,0,2,1:T(4,128)S(1)}, f32[3,1,1,512]{3,0,2,1:T(4,128)S(1)}, u32[]{:S(2)}, u32[]{:S(2)}) collective-permute-start(f32[3,1,1,512]{3,0,2,1:T(4,128)S(1)} %bitcast.260), channel_id=1, source_target_pairs={{32,0},{64,32},{96,64},{128,96},{160,128},{192,160},{224,192},{256... | collective-permute-start | bytes 18440 | tf_op jit(solution)/shard_map/ppermute | solution.py:26
  120.5 4.2 %collective-permute-start.8 = (f32[3,1,1,512]{3,0,2,1:T(4,128)S(1)}, f32[3,1,1,512]{3,0,2,1:T(4,128)S(1)}, u32[]{:S(2)}, u32[]{:S(2)}) collective-permute-start(f32[3,1,1,512]{3,0,2,1:T(4,128)S(1)} %bitcast.261), channel_id=1, source_target_pairs={{0,32},{32,64},{64,96},{96,128},{128,160},{160,192},{192,224},{224... | collective-permute-start | bytes 18440 | tf_op jit(solution)/shard_map/ppermute | solution.py:25
  124.8 7.5 %collective-permute-start.11 = (f32[3,3,1,512]{3,0,2,1:T(4,128)S(1)}, f32[3,3,1,512]{3,0,2,1:T(4,128)S(1)}, u32[]{:S(2)}, u32[]{:S(2)}) collective-permute-start(f32[3,3,1,512]{3,0,2,1:T(4,128)S(1)} %pad_maximum_fusion.5), channel_id=1, source_target_pairs={{1,0},{2,1},{3,2},{4,3},{5,4},{6,5},{7,6},{8,7},{9,8},{10,9},{11,1... | collective-permute-start | bytes 55304 | tf_op jit(solution)/shard_map/ppermute | solution.py:26
  126.0 6.9 %collective-permute-start.10 = (f32[3,3,1,512]{3,0,2,1:T(4,128)S(1)}, f32[3,3,1,512]{3,0,2,1:T(4,128)S(1)}, u32[]{:S(2)}, u32[]{:S(2)}) collective-permute-start(f32[3,3,1,512]{3,0,2,1:T(4,128)S(1)} %pad_maximum_fusion.5), channel_id=1, source_target_pairs={{0,1},{1,2},{2,3},{3,4},{4,5},{5,6},{6,7},{7,8},{8,9},{9,10},{10,1... | collective-permute-start | bytes 55304 | tf_op jit(solution)/shard_map/ppermute | solution.py:25
  165.9 142.6 %collective-permute-start.12 = (f32[3,3,512]{2,0,1:T(4,128)S(1)}, f32[3,3,512]{2,0,1:T(4,128)S(1)}, u32[]{:S(2)}, u32[]{:S(2)}) collective-permute-start(f32[3,3,512]{2,0,1:T(4,128)S(1)} %get-tuple-element.638), channel_id=1, source_target_pairs={{32,0},{64,32},{96,64},{128,96},{160,128},{192,160},{224,192},{256... | collective-permute-start | bytes 55304 | tf_op jit(solution)/shard_map/ppermute | solution.py:34
  167.8 140.7 %collective-permute-start.13 = (f32[3,3,512]{2,0,1:T(4,128)S(1)}, f32[3,3,512]{2,0,1:T(4,128)S(1)}, u32[]{:S(2)}, u32[]{:S(2)}) collective-permute-start(f32[3,3,512]{2,0,1:T(4,128)S(1)} %get-tuple-element.639), channel_id=1, source_target_pairs={{0,32},{32,64},{64,96},{96,128},{128,160},{160,192},{192,224},{224... | collective-permute-start | bytes 55304 | tf_op jit(solution)/shard_map/ppermute | solution.py:34
  172.3 145.2 %all-to-all-start.2 = ((f32[32,1,624]{2,1,0:T(1,128)}), f32[32,1,624]{2,1,0:T(1,128)S(1)}, u32[]{:S(2)}, u32[]{:S(2)}) async-start(f32[32,1,624]{2,1,0:T(1,128)} %reshape.533), calls=%async_computation.2 | async-start | bytes 163840 | tf_op jit(solution)/shard_map/all_to_all | solution.py:39
  319.3 16.7 %all-to-all-start.3 = ((f32[16,1,624]{2,1,0:T(1,128)}), f32[16,1,624]{2,1,0:T(1,128)S(1)}, u32[]{:S(2)}, u32[]{:S(2)}) async-start(f32[16,1,624]{2,1,0:T(1,128)} %reshape.535), calls=%async_computation.3 | async-start | bytes 81920 | tf_op jit(solution)/shard_map/all_to_all | solution.py:39
  328.5 18.9 %collective-permute-start.14 = (f32[3,512]{1,0:T(4,128)S(1)}, f32[3,512]{1,0:T(4,128)S(1)}, u32[]{:S(2)}, u32[]{:S(2)}) collective-permute-start(f32[3,512]{1,0:T(4,128)S(1)} %get-tuple-element.642), channel_id=1, source_target_pairs={{1,0},{2,1},{3,2},{4,3},{5,4},{6,5},{7,6},{8,7},{9,8},{10,9},{11,1... | collective-permute-start | bytes 18440 | tf_op jit(solution)/shard_map/ppermute | solution.py:34
  329.8 17.6 %collective-permute-start.15 = (f32[3,512]{1,0:T(4,128)S(1)}, f32[3,512]{1,0:T(4,128)S(1)}, u32[]{:S(2)}, u32[]{:S(2)}) collective-permute-start(f32[3,512]{1,0:T(4,128)S(1)} %get-tuple-element.643), channel_id=1, source_target_pairs={{0,1},{1,2},{2,3},{3,4},{4,5},{5,6},{6,7},{7,8},{8,9},{9,10},{10,1... | collective-permute-start | bytes 18440 | tf_op jit(solution)/shard_map/ppermute | solution.py:34
where the time goes:
time: 349 us
  starting transfers between devices  233 us (67%)
  other arithmetic  45.5 us (13%)
  local copies, waits for them, and re-layouts  35.5 us (10%)
  matrix products  17.2 us (5%)
  waiting for transfers between devices  13.6 us (4%)
    all_to_all x4, starting transfers between devices, from_everyone(): lax.all_to_all(jnp.broadcast_to(x[None], (peers, *x.shape)), axis, 0, 0,...  180 us
    ppermute x8, starting transfers between devices, shifted(): return lax.ppermute(block, axis, route)  24.2 us
    ppermute x4, starting transfers between devices, padded(): before = lax.ppermute(last, axis, up)  15.3 us
    ppermute x4, starting transfers between devices, padded(): after = lax.ppermute(initial, axis, down)  13.6 us
    scatter-add x20, other arithmetic, turn(): return acc.at[:, first_blk].add(force_a).at[:, second_blk].add(force_b)  12.9 us
    all_to_all x4, waiting for transfers between devices, from_everyone(): lax.all_to_all(jnp.broadcast_to(x[None], (peers, *x.shape)), axis, 0, 0,...  11.1 us
    dot_general x8, matrix products, visit(): jnp.einsum('kabc,kn->abcn', mpart[12:39].reshape(3, 3, 3, 64), burg, prec...  9.49 us
  transfers between devices with their start and end apart: 20, of which 6 were waited for; matrix products, arithmetic and copies ran while one was open for 17% of the time, Pallas kernels for 0%

commit v1 on v0

v1 whole, which is shorter than its diff:
```python
import functools
import math

import jax
import jax.numpy as jnp
from jax import lax
from jax.experimental import pallas as pl
from jax.experimental.pallas import tpu as pltpu
from jax.sharding import PartitionSpec as P

MESH = pl.DeviceIdType.MESH
F32 = jnp.float32
BF16 = jnp.bfloat16

BLK = 4
LANES = 128
SLOTS = 64
OWN = 16
UNROLL = 4
core_far = 9.0
time_increment = 0.25
around = [(ds, de) for ds in (-1, 0, 1) for de in (-1, 0, 1) if (ds, de) != (0, 0)]


def split3(x):
    hi = x.astype(BF16).astype(F32)
    rest = x - hi
    mid = rest.astype(BF16).astype(F32)
    return hi, mid, rest - mid


def left_stack(parts):
    hi, mid, lo = parts
    return jnp.concatenate([hi, hi, mid, hi, mid, lo], axis=0)


def right_stack(parts):
    hi, mid, lo = parts
    return jnp.concatenate([hi, mid, hi, lo, mid, hi], axis=0)


def mm(a, b, ca=1, cb=0):
    return lax.dot_general(a, b, (((ca,), (cb,)), ((), ())), preferred_element_type=F32)


def iotas():
    row = lax.broadcasted_iota(jnp.int32, (8, LANES), 0)
    lane = lax.broadcasted_iota(jnp.int32, (8, LANES), 1)
    return row, lane


def step_kernel(
    n_slab,
    n_dom,
    far_scale,
    pos_ref,
    bur_ref,
    mob_ref,
    cells_ref,
    pairs_ref,
    count_ref,
    out_ref,
    idx_a,
    idx_b,
    onehot,
    onehot_t,
    own,
    window,
    left_feat,
    right_feat,
    sums_feat,
    pair_sums,
    give,
    given,
    mom_dom,
    mom_slab,
    feats,
    feats_split,
    bur_split,
    q_buf,
    far_buf,
    pos_rows,
    mob_rows,
    send_sem,
    recv_sem,
):
    s = lax.axis_index("slab")
    e = lax.axis_index("dom")
    halves = n_slab // 8
    row, lane = iotas()
    centre_x = (4 * s + 2).astype(F32)
    centre = jnp.where(row == 0, centre_x, jnp.where(row < 3, 4.0, 0.0))

    def peer(ds, de):
        return (lax.rem(s + ds + n_slab, n_slab), lax.rem(e + de + n_dom, n_dom))

    barrier = pltpu.get_barrier_semaphore()

    def greet(slab, dom):
        pl.semaphore_signal(barrier, inc=1, device_id=(slab, dom), device_id_type=MESH)

    def greet_dom(i, c):
        greet(s, lax.rem(e + i, n_dom))
        return c

    def greet_slab(i, c):
        greet(lax.rem(s + i, n_slab), e)
        return c

    lax.fori_loop(1, n_dom, greet_dom, 0)
    lax.fori_loop(1, n_slab, greet_slab, 0)
    for ds, de in around:
        if ds != 0 and de != 0:
            greet(*peer(ds, de))

    device = s * n_dom + e
    used = count_ref[0]

    def place(t, c):
        first = pairs_ref[2 * t]
        second = pairs_ref[2 * t + 1]
        owner = second // BLK
        row_off = owner // n_dom - s + 1
        col_off = owner % n_dom - e + 1
        ia = jnp.clip(first - device * BLK, 0, BLK - 1)
        ib = jnp.clip((row_off * 3 + col_off) * BLK + second % BLK, 0, 9 * BLK - 1)
        idx_a[t] = ia
        idx_b[t] = ib
        live = t < used
        to_a = jnp.where(live, OWN + ia, LANES - 1)
        to_b = jnp.where(live, ib, LANES - 1)
        one_lane = lax.broadcasted_iota(jnp.int32, (1, LANES), 1)
        onehot[pl.ds(t, 1), :] = jnp.where(one_lane == to_a, 1.0, 0.0)
        onehot[pl.ds(SLOTS + t, 1), :] = jnp.where(one_lane == to_b, 1.0, 0.0)
        return c

    lax.fori_loop(0, SLOTS, place, 0)
    onehot_t[...] = jnp.transpose(onehot[...])[:48].astype(BF16)

    bur_tiles = []
    for b in range(BLK):
        cols = slice(b * LANES, (b + 1) * LANES)
        bur = bur_ref[:, cols]
        bur_tiles.append(bur)
        for c in range(3):
            pos_rows[c, b : b + 1, :] = pos_ref[c : c + 1, cols]
        mob_rows[b : b + 1, :] = mob_ref[:, cols]
        padded = jnp.concatenate([bur, jnp.zeros((5, LANES), F32)], axis=0)
        bur_split[:, cols] = right_stack(split3(padded)).astype(BF16)
    feats[...] = jnp.zeros(feats.shape, F32)

    def local_moments(phase):
        sums = [jnp.zeros((8, LANES), F32) for _ in range(4)]
        for b in range(BLK):
            tile = own[phase, b]
            inside = cells_ref[b] - 16 * s
            zy = (2 * (inside // 4) + 1).astype(F32)
            zz = (2 * (inside % 4) + 1).astype(F32)
            d0 = tile[0:1] - centre_x
            d1 = tile[1:2] - zy
            d2 = tile[2:3] - zz
            one = jnp.ones((1, LANES), F32)
            mono = jnp.concatenate([one, d0, d1, d2, d0 * d0, d1 * d1, d2 * d2, d0 * d1], axis=0)
            more = jnp.concatenate([d0 * d2, d1 * d2, jnp.zeros((6, LANES), F32)], axis=0)
            spot = lane == 16 * row + inside
            for k in range(3):
                bk = tile[3 + k : 4 + k]
                m = jnp.sum(mono * bk, axis=1, keepdims=True)
                sums[k] = sums[k] + jnp.where(spot, m, 0.0)
                m = jnp.sum(more * bk, axis=1, keepdims=True)
                sums[3] = sums[3] + jnp.where(lane == 16 * (row + 2 * k) + inside, m, 0.0)
        rows = [jnp.sum(x, axis=0, keepdims=True) for x in sums]
        mom_dom[phase, e] = jnp.concatenate(rows, axis=0)

    def remote(src, dst, phase, kind, target):
        return pltpu.make_async_remote_copy(
            src_ref=src,
            dst_ref=dst,
            send_sem=send_sem.at[phase, kind],
            recv_sem=recv_sem.at[phase, kind],
            device_id=target,
            device_id_type=MESH,
        )

    def start_halo(phase):
        for ds, de in around:
            slot = (1 - ds) * 3 + (1 - de)
            dst = window.at[phase, pl.ds(slot * BLK, BLK)]
            remote(own.at[phase], dst, phase, 0, peer(ds, de)).start()

    def start_dom(phase):
        def go(i, c):
            mine = mom_dom.at[phase, e]
            remote(mine, mine, phase, 1, (s, lax.rem(e + i, n_dom))).start()
            return c

        lax.fori_loop(1, n_dom, go, 0)

    def start_slab(phase):
        def go(i, c):
            mine = mom_slab.at[phase, s]
            remote(mine, mine, phase, 2, (lax.rem(s + i, n_slab), e)).start()
            return c

        lax.fori_loop(1, n_slab, go, 0)

    def start_give(phase):
        for ds, de in around:
            d = (ds + 1) * 3 + de + 1
            remote(give.at[phase, d], given.at[phase, 8 - d], phase, 3, peer(ds, de)).start()

    def extent(phase, kind):
        return (
            window.at[phase, pl.ds(0, 8 * BLK)],
            mom_dom.at[phase, pl.ds(0, n_dom - 1)],
            mom_slab.at[phase, pl.ds(0, n_slab - 1)],
            given.at[phase, pl.ds(0, 8)],
        )[kind]

    def all_of(phase, kind):
        whole = extent(phase, kind)
        return remote(whole, whole, phase, kind, peer(0, 1))

    def prepare(phase):
        def one(w, c):
            x = window[phase, w] - centre
            n = jnp.sum(jnp.where(row < 3, x * x, 0.0), axis=0, keepdims=True)
            mixed = jnp.where(row < 6, x, jnp.where(row == 6, n, 1.0))
            hi, mid, lo = split3(mixed)
            other = jnp.where(
                row < 3, -2.0 * x, jnp.where(row == 7, n + 0.25, jnp.where(row == 6, 1.0, 0.0))
            )
            right_feat[w, :, 0:LANES] = right_stack(split3(other)).astype(BF16)
            is_b = (row >= 3) & (row < 6)
            bs = [jnp.where(is_b, part, 0.0) for part in (hi, mid, lo)]
            right_feat[w, :, LANES : 2 * LANES] = right_stack(bs).astype(BF16)
            sums_feat[w] = jnp.concatenate([hi, mid], axis=0).astype(BF16)
            return c

        lax.fori_loop(0, 9 * BLK, one, 0, unroll=2)
        for b in range(BLK):
            x = own[phase, b] - centre
            n = jnp.sum(jnp.where(row < 3, x * x, 0.0), axis=0, keepdims=True)
            mixed = jnp.where(row < 6, x, jnp.where(row == 6, n, 1.0))
            left_feat[b] = jnp.transpose(left_stack(split3(mixed))).astype(BF16)

    def near(begin, end):
        def pair(t):
            ia = idx_a[t]
            ib = idx_b[t]
            both = mm(left_feat[ia], right_feat[ib])
            close = both[:, 0:LANES]
            coef = both[:, LANES : 2 * LANES]
            r1 = lax.rsqrt(close)
            r2 = lax.rsqrt(close + (core_far - 0.25))
            w = coef * (r1 * r1 * r1 - r2 * r2 * r2)
            hi = w.astype(BF16)
            lo = (w - hi.astype(F32)).astype(BF16)
            fa = sums_feat[OWN + ia]
            fb = sums_feat[ib]
            on_b = mm(fa, hi) + mm(fa, lo)
            on_a = mm(fb, hi, 1, 1) + mm(fb, lo, 1, 1)
            on_a = on_a[0:8] + on_a[8:16]
            on_b = on_b[0:8] + on_b[8:16]
            for i, r in enumerate((0, 1, 2, 7)):
                pair_sums[i, pl.ds(t, 1), :] = on_a[r : r + 1]
                pair_sums[i, pl.ds(SLOTS + t, 1), :] = on_b[r : r + 1]

        def turn(i, c):
            for u in range(UNROLL):
                pair(i * UNROLL + u)
            return c

        lax.fori_loop(begin // UNROLL, end // UNROLL, turn, 0)

    def collect(phase):
        chosen = onehot_t[...]
        acc = []
        for i in range(4):
            hi, mid, lo = split3(pair_sums[i])
            acc.append(mm(chosen, hi.astype(BF16)) + mm(chosen, mid.astype(BF16)) + mm(chosen, lo.astype(BF16)))
        blocks = lax.broadcasted_iota(jnp.int32, (48, LANES), 0)
        shift = (4 * (1 - blocks // 12)).astype(F32)
        acc[0] = acc[0] + shift * acc[3]
        for d in range(9):
            for i in range(4):
                give[phase, d, i] = acc[i][d * BLK : (d + 1) * BLK]

    def swap_groups(x):
        for d in (1, 2, 4):
            up = pltpu.roll(pltpu.roll(x, 8 - d, 0), 16 * d, 1)
            down = pltpu.roll(pltpu.roll(x, d, 0), LANES - 16 * d, 1)
            rbit = (row // d) % 2
            gbit = (lane // (16 * d)) % 2
            x = jnp.where(rbit == gbit, x, jnp.where(rbit == 0, up, down))
        return x

    def far(phase, half):
        for q in range(4):
            rows = jnp.concatenate(
                [mom_slab[phase, half * 8 + j, q : q + 1, :] for j in range(8)], axis=0
            )
            x = swap_groups(rows)
            if q < 3:
                for f in range(8):
                    feats[f, q : q + 1, :] = x[f : f + 1] * (1.0 if f < 4 else 3.0)
                feats[10, q : q + 1, :] = -1.5 * (x[4:5] + x[5:6] + x[6:7])
            else:
                for k in range(3):
                    for f in (8, 9):
                        j = 2 * k + f - 8
                        feats[f, k : k + 1, :] = x[j : j + 1] * 3.0
        for f in range(11):
            stacked = left_stack(split3(feats[f])).astype(BF16)
            q_buf[f] = mm(stacked, bur_split[...], 0, 0)

        zz = (2 * (row % 4) + 1).astype(F32)

        def group(g, acc):
            acc = list(acc)
            zx = (4 * (half * 8 + g // 2) + 2).astype(F32)
            zy = (2 * (2 * (g % 2) + row // 4) + 1).astype(F32)
            for t in range(BLK):
                cols = slice(t * LANES, (t + 1) * LANES)
                q = [q_buf[f, pl.ds(pl.multiple_of(8 * g, 8), 8), cols] for f in range(11)]
                dx = jnp.broadcast_to(far_buf[0, t : t + 1, :] - zx, (8, LANES))
                dy = far_buf[1, t : t + 1, :] - zy
                dz = far_buf[2, t : t + 1, :] - zz
                rs = lax.rsqrt(dx * dx + (dy * dy + dz * dz + core_far))
                i2 = rs * rs
                i3 = rs * i2
                qr = q[1] * dx + q[2] * dy + q[3] * dz
                tx = q[4] * dx + q[7] * dy + q[8] * dz
                ty = q[7] * dx + q[5] * dy + q[9] * dz
                tz = q[8] * dx + q[9] * dy + q[6] * dz
                rqr = tx * dx + ty * dy + tz * dz
                scal = q[0] + i2 * (3.0 * qr + q[10] + 2.5 * i2 * rqr)
                acc[t] = acc[t] + i3 * (dx * scal - q[1] - i2 * tx)
                acc[4 + t] = acc[4 + t] + i3 * (dy * scal - q[2] - i2 * ty)
                acc[8 + t] = acc[8 + t] + i3 * (dz * scal - q[3] - i2 * tz)
            return tuple(acc)

        zero = jnp.zeros((8, LANES), F32)
        return lax.fori_loop(0, 16, group, (zero,) * 12)

    def speed(phase):
        p = [far_buf[c] for c in range(3)]
        prepare(phase)
        near(0, SLOTS // 2)
        all_of(phase, 1).wait_recv()
        mom_slab[phase, s] = jnp.sum(mom_dom[phase], axis=0)
        start_slab(phase)
        near(SLOTS // 2, SLOTS)
        collect(phase)
        start_give(phase)
        all_of(phase, 2).wait_recv()
        total = None
        for half in range(halves):
            acc = far(phase, half)
            total = acc if total is None else [x + y for x, y in zip(total, acc)]
        all_of(phase, 3).wait_recv()
        got = [give[phase, 4, i] for i in range(4)]
        for d in range(9):
            if d != 4:
                got = [got[i] + given[phase, d, i] for i in range(4)]
        v = []
        for c in range(3):
            fars = [jnp.sum(total[4 * c + t], axis=0, keepdims=True) for t in range(BLK)]
            near_c = (p[c] - (centre_x if c == 0 else 4.0)) * got[3] - got[c]
            v.append(mob_rows[...] * (far_scale * jnp.concatenate(fars, axis=0) + near_c))
        return v

    def publish(phase, p):
        for b in range(BLK):
            tile = jnp.concatenate(
                [x[b : b + 1] for x in p] + [bur_tiles[b], jnp.zeros((2, LANES), F32)], axis=0
            )
            own[phase, b] = tile
            window[phase, OWN + b] = tile
        for c in range(3):
            far_buf[c] = p[c]
        local_moments(phase)

    first_p = [pos_rows[c] for c in range(3)]
    publish(0, first_p)
    pl.semaphore_wait(barrier, n_dom - 1 + n_slab - 1 + 4)
    start_halo(0)
    start_dom(0)
    all_of(0, 0).wait_recv()
    first_v = speed(0)
    second_p = [p + time_increment * v for p, v in zip(first_p, first_v)]
    publish(1, second_p)
    start_halo(1)
    start_dom(1)
    all_of(1, 0).wait_recv()
    second_v = speed(1)
    for c in range(3):
        both = first_v[c] + second_v[c]
        for b in range(BLK):
            out_ref[c : c + 1, b * LANES : (b + 1) * LANES] = both[b : b + 1]
    for phase in range(2):
        for kind in range(4):
            all_of(phase, kind).wait_send()


def solution(mesh):
    n_slab = mesh.shape["slab"]
    n_dom = mesh.shape["dom"]

    def body(positions, burgers, mobility, block_cells, pairs, pair_count):
        segs = positions.shape[1]
        far_scale = math.sqrt(16 * n_slab / (segs * n_slab * n_dom))
        vmem = pl.BlockSpec(memory_space=pltpu.VMEM)
        smem = pl.BlockSpec(memory_space=pltpu.SMEM)
        total = pl.pallas_call(
            functools.partial(step_kernel, n_slab, n_dom, far_scale),
            out_shape=jax.ShapeDtypeStruct((3, segs), F32),
            in_specs=[vmem, vmem, vmem, smem, smem, smem],
            out_specs=vmem,
            scratch_shapes=[
                pltpu.SMEM((SLOTS,), jnp.int32),
                pltpu.SMEM((SLOTS,), jnp.int32),
                pltpu.VMEM((2 * SLOTS, LANES), F32),
                pltpu.VMEM((48, 2 * SLOTS), BF16),
                pltpu.VMEM((2, BLK, 8, LANES), F32),
                pltpu.VMEM((2, 9 * BLK, 8, LANES), F32),
                pltpu.VMEM((BLK, LANES, 48), BF16),
                pltpu.VMEM((9 * BLK, 48, 2 * LANES), BF16),
                pltpu.VMEM((9 * BLK, 16, LANES), BF16),
                pltpu.VMEM((4, 2 * SLOTS, LANES), F32),
                pltpu.VMEM((2, 9, 4, BLK, LANES), F32),
                pltpu.VMEM((2, 9, 4, BLK, LANES), F32),
                pltpu.VMEM((2, n_dom, 4, LANES), F32),
                pltpu.VMEM((2, n_slab, 4, LANES), F32),
                pltpu.VMEM((11, 8, LANES), F32),
                pltpu.VMEM((11, 48, LANES), BF16),
                pltpu.VMEM((48, segs), BF16),
                pltpu.VMEM((11, LANES, segs), F32),
                pltpu.VMEM((3, BLK, LANES), F32),
                pltpu.VMEM((3, BLK, LANES), F32),
                pltpu.VMEM((BLK, LANES), F32),
                pltpu.SemaphoreType.DMA((2, 4)),
                pltpu.SemaphoreType.DMA((2, 4)),
            ],
            compiler_params=pltpu.CompilerParams(collective_id=0, has_side_effects=True),
        )(positions, burgers, mobility.reshape(1, -1), block_cells, pairs.reshape(-1), pair_count)
        return (positions + 0.5 * time_increment * total, 0.5 * total)

    placed = (
        P(None, ("slab", "dom")),
        P(None, ("slab", "dom")),
        P(("slab", "dom")),
        P(("slab", "dom")),
        P(("slab", "dom"), None),
        P(("slab", "dom")),
    )
    return jax.shard_map(
        body,
        mesh=mesh,
        in_specs=placed,
        out_specs=(P(None, ("slab", "dom")), P(None, ("slab", "dom"))),
        check_vma=False,
    )
```

time: 349 us -> 74.5 us (0.21)
  starting transfers between devices: 233 us -> 0 us
  Pallas kernels: 0 us -> 70.2 us
  other arithmetic: 45.5 us -> 1.3 us
  local copies, waits for them, and re-layouts: 35.5 us -> 1.43 us
  matrix products: 17.2 us -> 0 us
  waiting for transfers between devices: 13.6 us -> 0 us
    all_to_all x4 -> x0, starting transfers between devices: 180 us -> none  [from_everyone(): lax.all_to_all(jnp.broadcast_to(x[None], (peers, *x.shape)), axis, 0, 0,...]
    pallas_call x0 -> x1, Pallas kernels: none -> 70.2 us  [body(): pl.pallas_call(functools.partial(step_kernel, n_slab, n_dom, far_scale),...]
    ppermute x16 -> x0, starting transfers between devices: 53.1 us -> none  [the longest x8 24.2 us: shifted(): return lax.ppermute(block, axis, route)]
    gather x90 -> x0, local copies, waits for them, and re-layouts: 28.7 us -> none  [the longest x20 5.77 us: turn(): pos_win[:, second_blk]]
    dot_general x26 -> x0, matrix products: 17.2 us -> none  [the longest x8 9.49 us: visit(): jnp.einsum('kabc,kn->abcn', mpart[12:39].reshape(3, 3, 3, 64), burg, prec...]
    scatter-add x20 -> x0, other arithmetic: 12.9 us -> none  [turn(): return acc.at[:, first_blk].add(force_a).at[:, second_blk].add(force_b)]
    all_to_all x4 -> x0, waiting for transfers between devices: 11.1 us -> none  [from_everyone(): lax.all_to_all(jnp.broadcast_to(x[None], (peers, *x.shape)), axis, 0, 0,...]
    reduce_sum x32 -> x0, other arithmetic: 9.68 us -> none  [the longest x10 5.37 us: pair_forces(): return (jnp.sum(wr, axis=3), -jnp.sum(wr, axis=2))]
  transfers between devices with their start and end apart: 20 -> 0, of which waited for: 6 -> 0; matrix products, arithmetic and copies ran while one was open for 17% -> 0% of each run, Pallas kernels for 0% -> 0%
where the time goes in v1:
time: 74.5 us; the launch traced here: 74.3 us
  Pallas kernels  70.2 us (94%)
  local copies, waits for them, and re-layouts  1.43 us (2%)
  between operations  1.31 us (2%)
  other arithmetic  1.3 us (2%)
    pallas_call x1, Pallas kernels, body(): pl.pallas_call(functools.partial(step_kernel, n_slab, n_dom, far_scale),...  70.2 us

profile of v1, /device:TPU:1, one launch (start us, length us, event | category | flops | bytes accessed | tf_op | source)
XLA Modules:
  0.0 74.3 jit_solution(15581226925203418357)
XLA Ops:
  0.6 0.8 %copy.9 = s32[64,2]{1,0:T(8,128)S(1)} copy(s32[64,2]{0,1:T(2,128)} %param.10) | data formatting | bytes 1024 | tf_op args[4]
  1.4 0.7 reshape.11.pairs_ref
  2.7 0.0 copy-start
  2.7 70.2 %shard_map.77 = f32[3,512]{1,0:T(4,128)} custom-call(f32[3,512]{1,0:T(4,128)} %pos_ref.1, f32[3,512]{1,0:T(4,128)} %bur_ref.1, f32[1,512]{1,0:T(1,128)} %bitcast.1, s32[4]{0:T(128)} %cells_ref.1, s32[128]{0:T(128)} %reshape.11.pairs_ref, s32[1]{0:T(128)S(6)} %copy.10.count_ref), custom_call_target="tpu_custom_call" | custom-call | tf_op jit(solution)/shard_map/pallas_call | solution.py:415
  72.9 0.0 copy-done
  73.0 1.3 %broadcast_multiply_fusion = (f32[3,512]{1,0:T(4,128)}, f32[3,512]{1,0:T(4,128)}) fusion(f32[3,512]{1,0:T(4,128)} %shard_map.77, f32[3,512]{1,0:T(4,128)S(1)} %copy-done), kind=kLoop, calls=%fused_computation.1 | loop fusion | flops 4608 | bytes 24576 | tf_op jit(solution)/shard_map/mul | solution.py:447
Async XLA Ops:
  2.7 70.2 %copy-start = (f32[3,512]{1,0:T(4,128)S(1)}, f32[3,512]{1,0:T(4,128)}, u32[]{:S(2)}) copy-start(f32[3,512]{1,0:T(4,128)} %pos_ref.1) | copy-start | bytes 18436

commit v2 on v1

--- a/solution.py
+++ b/solution.py
@@ -16,7 +16,8 @@
 LANES = 128
 SLOTS = 64
 OWN = 16
-UNROLL = 4
+UNROLL = 8
+FIRST_PART = 24
 core_far = 9.0
 time_increment = 0.25
 around = [(ds, de) for ds in (-1, 0, 1) for de in (-1, 0, 1) if (ds, de) != (0, 0)]
@@ -66,16 +67,18 @@
     onehot_t,
     own,
     window,
+    own_next,
+    window_next,
     left_feat,
     right_feat,
     sums_feat,
     pair_sums,
     give,
     given,
-    mom_dom,
+    mom_y,
+    mom_xc,
     mom_slab,
     feats,
-    feats_split,
     bur_split,
     q_buf,
     far_buf,
@@ -94,31 +97,36 @@
     def peer(ds, de):
         return (lax.rem(s + ds + n_slab, n_slab), lax.rem(e + de + n_dom, n_dom))
 
+    ny = 8 if n_dom % 8 == 0 else n_dom
+    nx = n_dom // ny
+    nz = n_slab // 2
+    x, y, z, core = e // ny, e % ny, s // 2, s % 2
+    y_peers = [(s, x * ny + lax.rem(y + i, ny)) for i in range(1, ny)]
+    xc_peers = [
+        (2 * z + lax.rem(core + c, 2), lax.rem(x + i, nx) * ny + y)
+        for i in range(nx)
+        for c in range(2)
+        if (i, c) != (0, 0)
+    ]
+    z_peers = [(2 * lax.rem(z + i, nz) + core, e) for i in range(1, nz)]
+
     barrier = pltpu.get_barrier_semaphore()
 
     def greet(slab, dom):
         pl.semaphore_signal(barrier, inc=1, device_id=(slab, dom), device_id_type=MESH)
 
-    def greet_dom(i, c):
-        greet(s, lax.rem(e + i, n_dom))
-        return c
-
-    def greet_slab(i, c):
-        greet(lax.rem(s + i, n_slab), e)
-        return c
-
-    lax.fori_loop(1, n_dom, greet_dom, 0)
-    lax.fori_loop(1, n_slab, greet_slab, 0)
+    for group in (y_peers, xc_peers, z_peers):
+        for slab, dom in group:
+            greet(slab, dom)
     for ds, de in around:
-        if ds != 0 and de != 0:
-            greet(*peer(ds, de))
+        greet(*peer(ds, de))
 
     device = s * n_dom + e
     used = count_ref[0]
 
     def place(t, c):
-        first = pairs_ref[2 * t]
-        second = pairs_ref[2 * t + 1]
+        first = pairs_ref[0, t]
+        second = pairs_ref[1, t]
         owner = second // BLK
         row_off = owner // n_dom - s + 1
         col_off = owner % n_dom - e + 1
@@ -170,7 +178,7 @@
                 m = jnp.sum(more * bk, axis=1, keepdims=True)
                 sums[3] = sums[3] + jnp.where(lane == 16 * (row + 2 * k) + inside, m, 0.0)
         rows = [jnp.sum(x, axis=0, keepdims=True) for x in sums]
-        mom_dom[phase, e] = jnp.concatenate(rows, axis=0)
+        mom_y[phase, y] = jnp.concatenate(rows, axis=0)
 
     def remote(src, dst, phase, kind, target):
         return pltpu.make_async_remote_copy(
@@ -185,35 +193,44 @@
     def start_halo(phase):
         for ds, de in around:
             slot = (1 - ds) * 3 + (1 - de)
-            dst = window.at[phase, pl.ds(slot * BLK, BLK)]
-            remote(own.at[phase], dst, phase, 0, peer(ds, de)).start()
-
-    def start_dom(phase):
-        def go(i, c):
-            mine = mom_dom.at[phase, e]
-            remote(mine, mine, phase, 1, (s, lax.rem(e + i, n_dom))).start()
-            return c
-
-        lax.fori_loop(1, n_dom, go, 0)
-
-    def start_slab(phase):
-        def go(i, c):
-            mine = mom_slab.at[phase, s]
-            remote(mine, mine, phase, 2, (lax.rem(s + i, n_slab), e)).start()
-            return c
-
-        lax.fori_loop(1, n_slab, go, 0)
+            if phase == 0:
+                src, dst = own.at[0], window.at[pl.ds(slot * BLK, BLK)]
+            else:
+                src, dst = own_next, window_next.at[pl.ds(slot * 2, 2)]
+            remote(src, dst, phase, 0, peer(ds, de)).start()
+
+    def start_y(phase):
+        mine = mom_y.at[phase, y]
+        for target in y_peers:
+            remote(mine, mine, phase, 1, target).start()
+
+    def start_xc(phase):
+        all_of(phase, 1).wait_recv()
+        mom_xc[phase, 2 * x + core] = jnp.sum(mom_y[phase], axis=0)
+        mine = mom_xc.at[phase, 2 * x + core]
+        for target in xc_peers:
+            remote(mine, mine, phase, 2, target).start()
+
+    def start_z(phase):
+        all_of(phase, 2).wait_recv()
+        for c in range(2):
+            parts = [mom_xc[phase, 2 * i + c] for i in range(nx)]
+            mom_slab[phase, 2 * z + c] = sum(parts[1:], parts[0])
+        mine = mom_slab.at[phase, pl.ds(2 * z, 2)]
+        for target in z_peers:
+            remote(mine, mine, phase, 3, target).start()
 
     def start_give(phase):
         for ds, de in around:
             d = (ds + 1) * 3 + de + 1
-            remote(give.at[phase, d], given.at[phase, 8 - d], phase, 3, peer(ds, de)).start()
+            remote(give.at[phase, d], given.at[phase, 8 - d], phase, 4, peer(ds, de)).start()
 
     def extent(phase, kind):
         return (
-            window.at[phase, pl.ds(0, 8 * BLK)],
-            mom_dom.at[phase, pl.ds(0, n_dom - 1)],
-            mom_slab.at[phase, pl.ds(0, n_slab - 1)],
+            window.at[pl.ds(0, 8 * BLK)] if phase == 0 else window_next.at[pl.ds(0, 16)],
+            mom_y.at[phase, pl.ds(0, ny - 1)],
+            mom_xc.at[phase, pl.ds(0, 2 * nx - 1)],
+            mom_slab.at[phase, pl.ds(0, 2 * (nz - 1))],
             given.at[phase, pl.ds(0, 8)],
         )[kind]
 
@@ -222,26 +239,36 @@
         return remote(whole, whole, phase, kind, peer(0, 1))
 
     def prepare(phase):
-        def one(w, c):
-            x = window[phase, w] - centre
-            n = jnp.sum(jnp.where(row < 3, x * x, 0.0), axis=0, keepdims=True)
-            mixed = jnp.where(row < 6, x, jnp.where(row == 6, n, 1.0))
+        def block(w, tile):
+            r = tile - centre
+            n = jnp.sum(jnp.where(row < 3, r * r, 0.0), axis=0, keepdims=True)
+            mixed = jnp.where(row < 6, r, jnp.where(row == 6, n, 1.0))
             hi, mid, lo = split3(mixed)
             other = jnp.where(
-                row < 3, -2.0 * x, jnp.where(row == 7, n + 0.25, jnp.where(row == 6, 1.0, 0.0))
+                row < 3, -2.0 * r, jnp.where(row == 7, n + 0.25, jnp.where(row == 6, 1.0, 0.0))
             )
             right_feat[w, :, 0:LANES] = right_stack(split3(other)).astype(BF16)
-            is_b = (row >= 3) & (row < 6)
-            bs = [jnp.where(is_b, part, 0.0) for part in (hi, mid, lo)]
-            right_feat[w, :, LANES : 2 * LANES] = right_stack(bs).astype(BF16)
+            if phase == 0:
+                is_b = (row >= 3) & (row < 6)
+                bs = [jnp.where(is_b, part, 0.0) for part in (hi, mid, lo)]
+                right_feat[w, :, LANES : 2 * LANES] = right_stack(bs).astype(BF16)
             sums_feat[w] = jnp.concatenate([hi, mid], axis=0).astype(BF16)
+
+        def two(i, c):
+            if phase == 0:
+                first, second = window[2 * i], window[2 * i + 1]
+            else:
+                first = window_next[i]
+                second = pltpu.roll(first, 4, 0)
+            block(2 * i, first)
+            block(2 * i + 1, second)
             return c
 
-        lax.fori_loop(0, 9 * BLK, one, 0, unroll=2)
+        lax.fori_loop(0, 9 * BLK // 2, two, 0)
         for b in range(BLK):
-            x = own[phase, b] - centre
-            n = jnp.sum(jnp.where(row < 3, x * x, 0.0), axis=0, keepdims=True)
-            mixed = jnp.where(row < 6, x, jnp.where(row == 6, n, 1.0))
+            r = own[phase, b] - centre
+            n = jnp.sum(jnp.where(row < 3, r * r, 0.0), axis=0, keepdims=True)
+            mixed = jnp.where(row < 6, r, jnp.where(row == 6, n, 1.0))
             left_feat[b] = jnp.transpose(left_stack(split3(mixed))).astype(BF16)
 
     def near(begin, end):
@@ -258,8 +285,10 @@
             lo = (w - hi.astype(F32)).astype(BF16)
             fa = sums_feat[OWN + ia]
             fb = sums_feat[ib]
-            on_b = mm(fa, hi) + mm(fa, lo)
-            on_a = mm(fb, hi, 1, 1) + mm(fb, lo, 1, 1)
+            for_b = jnp.concatenate([hi, lo], axis=0)
+            for_a = jnp.concatenate([jnp.transpose(hi), jnp.transpose(lo)], axis=0)
+            on_b = mm(jnp.concatenate([fa, fa], axis=1), for_b)
+            on_a = mm(jnp.concatenate([fb, fb], axis=1), for_a)
             on_a = on_a[0:8] + on_a[8:16]
             on_b = on_b[0:8] + on_b[8:16]
             for i, r in enumerate((0, 1, 2, 7)):
@@ -286,30 +315,30 @@
             for i in range(4):
                 give[phase, d, i] = acc[i][d * BLK : (d + 1) * BLK]
 
-    def swap_groups(x):
+    def swap_groups(m):
         for d in (1, 2, 4):
-            up = pltpu.roll(pltpu.roll(x, 8 - d, 0), 16 * d, 1)
-            down = pltpu.roll(pltpu.roll(x, d, 0), LANES - 16 * d, 1)
+            up = pltpu.roll(pltpu.roll(m, 8 - d, 0), 16 * d, 1)
+            down = pltpu.roll(pltpu.roll(m, d, 0), LANES - 16 * d, 1)
             rbit = (row // d) % 2
             gbit = (lane // (16 * d)) % 2
-            x = jnp.where(rbit == gbit, x, jnp.where(rbit == 0, up, down))
-        return x
+            m = jnp.where(rbit == gbit, m, jnp.where(rbit == 0, up, down))
+        return m
 
     def far(phase, half):
         for q in range(4):
             rows = jnp.concatenate(
                 [mom_slab[phase, half * 8 + j, q : q + 1, :] for j in range(8)], axis=0
             )
-            x = swap_groups(rows)
+            m = swap_groups(rows)
             if q < 3:
                 for f in range(8):
-                    feats[f, q : q + 1, :] = x[f : f + 1] * (1.0 if f < 4 else 3.0)
-                feats[10, q : q + 1, :] = -1.5 * (x[4:5] + x[5:6] + x[6:7])
+                    feats[f, q : q + 1, :] = m[f : f + 1] * (1.0 if f < 4 else 3.0)
+                feats[10, q : q + 1, :] = -1.5 * (m[4:5] + m[5:6] + m[6:7])
             else:
                 for k in range(3):
                     for f in (8, 9):
                         j = 2 * k + f - 8
-                        feats[f, k : k + 1, :] = x[j : j + 1] * 3.0
+                        feats[f, k : k + 1, :] = m[j : j + 1] * 3.0
         for f in range(11):
             stacked = left_stack(split3(feats[f])).astype(BF16)
             q_buf[f] = mm(stacked, bur_split[...], 0, 0)
@@ -345,20 +374,20 @@
 
     def speed(phase):
         p = [far_buf[c] for c in range(3)]
+        start_xc(phase)
+        all_of(phase, 0).wait_recv()
         prepare(phase)
-        near(0, SLOTS // 2)
-        all_of(phase, 1).wait_recv()
-        mom_slab[phase, s] = jnp.sum(mom_dom[phase], axis=0)
-        start_slab(phase)
-        near(SLOTS // 2, SLOTS)
+        near(0, FIRST_PART)
+        start_z(phase)
+        near(FIRST_PART, SLOTS)
         collect(phase)
         start_give(phase)
-        all_of(phase, 2).wait_recv()
+        all_of(phase, 3).wait_recv()
         total = None
         for half in range(halves):
             acc = far(phase, half)
-            total = acc if total is None else [x + y for x, y in zip(total, acc)]
-        all_of(phase, 3).wait_recv()
+            total = acc if total is None else [u + w for u, w in zip(total, acc)]
+        all_of(phase, 4).wait_recv()
         got = [give[phase, 4, i] for i in range(4)]
         for d in range(9):
             if d != 4:
@@ -373,33 +402,41 @@
     def publish(phase, p):
         for b in range(BLK):
             tile = jnp.concatenate(
-                [x[b : b + 1] for x in p] + [bur_tiles[b], jnp.zeros((2, LANES), F32)], axis=0
+                [q[b : b + 1] for q in p] + [bur_tiles[b], jnp.zeros((2, LANES), F32)], axis=0
             )
             own[phase, b] = tile
-            window[phase, OWN + b] = tile
+            if phase == 0:
+                window[OWN + b] = tile
+        if phase == 1:
+            blank = jnp.zeros((1, LANES), F32)
+            for half in range(2):
+                rows = []
+                for b in (2 * half, 2 * half + 1):
+                    rows += [q[b : b + 1] for q in p] + [blank]
+                packed = jnp.concatenate(rows, axis=0)
+                own_next[half] = packed
+                window_next[OWN // 2 + half] = packed
         for c in range(3):
             far_buf[c] = p[c]
         local_moments(phase)
 
     first_p = [pos_rows[c] for c in range(3)]
     publish(0, first_p)
-    pl.semaphore_wait(barrier, n_dom - 1 + n_slab - 1 + 4)
+    pl.semaphore_wait(barrier, len(y_peers) + len(xc_peers) + len(z_peers) + len(around))
+    start_y(0)
     start_halo(0)
-    start_dom(0)
-    all_of(0, 0).wait_recv()
     first_v = speed(0)
     second_p = [p + time_increment * v for p, v in zip(first_p, first_v)]
     publish(1, second_p)
+    start_y(1)
     start_halo(1)
-    start_dom(1)
-    all_of(1, 0).wait_recv()
     second_v = speed(1)
     for c in range(3):
         both = first_v[c] + second_v[c]
         for b in range(BLK):
             out_ref[c : c + 1, b * LANES : (b + 1) * LANES] = both[b : b + 1]
     for phase in range(2):
-        for kind in range(4):
+        for kind in range(5):
             all_of(phase, kind).wait_send()
 
 
@@ -423,27 +460,29 @@
                 pltpu.VMEM((2 * SLOTS, LANES), F32),
                 pltpu.VMEM((48, 2 * SLOTS), BF16),
                 pltpu.VMEM((2, BLK, 8, LANES), F32),
-                pltpu.VMEM((2, 9 * BLK, 8, LANES), F32),
+                pltpu.VMEM((9 * BLK, 8, LANES), F32),
+                pltpu.VMEM((2, 8, LANES), F32),
+                pltpu.VMEM((18, 8, LANES), F32),
                 pltpu.VMEM((BLK, LANES, 48), BF16),
                 pltpu.VMEM((9 * BLK, 48, 2 * LANES), BF16),
                 pltpu.VMEM((9 * BLK, 16, LANES), BF16),
                 pltpu.VMEM((4, 2 * SLOTS, LANES), F32),
                 pltpu.VMEM((2, 9, 4, BLK, LANES), F32),
                 pltpu.VMEM((2, 9, 4, BLK, LANES), F32),
-                pltpu.VMEM((2, n_dom, 4, LANES), F32),
+                pltpu.VMEM((2, 8 if n_dom % 8 == 0 else n_dom, 4, LANES), F32),
+                pltpu.VMEM((2, 2 * (n_dom // 8 if n_dom % 8 == 0 else 1), 4, LANES), F32),
                 pltpu.VMEM((2, n_slab, 4, LANES), F32),
                 pltpu.VMEM((11, 8, LANES), F32),
-                pltpu.VMEM((11, 48, LANES), BF16),
                 pltpu.VMEM((48, segs), BF16),
                 pltpu.VMEM((11, LANES, segs), F32),
                 pltpu.VMEM((3, BLK, LANES), F32),
                 pltpu.VMEM((3, BLK, LANES), F32),
                 pltpu.VMEM((BLK, LANES), F32),
-                pltpu.SemaphoreType.DMA((2, 4)),
-                pltpu.SemaphoreType.DMA((2, 4)),
+                pltpu.SemaphoreType.DMA((2, 5)),
+                pltpu.SemaphoreType.DMA((2, 5)),
             ],
             compiler_params=pltpu.CompilerParams(collective_id=0, has_side_effects=True),
-        )(positions, burgers, mobility.reshape(1, -1), block_cells, pairs.reshape(-1), pair_count)
+        )(positions, burgers, mobility.reshape(1, -1), block_cells, pairs.T, pair_count)
         return (positions + 0.5 * time_increment * total, 0.5 * total)
 
     placed = (

time: 74.5 us -> 51.7 us (0.69)
  Pallas kernels: 70.2 us -> 48.9 us
  local copies, waits for them, and re-layouts: 1.43 us -> 0.01 us
    pallas_call x1, Pallas kernels: 70.2 us -> 48.9 us  [body(): pl.pallas_call(functools.partial(step_kernel, n_slab, n_dom, far_scale),...]
    unnamed x3 -> x2, local copies, waits for them, and re-layouts: 0.78 us -> 0.01 us
where the time goes in v2:
time: 51.7 us; the launch traced here: 51.5 us
  Pallas kernels  48.9 us (95%)
  other arithmetic  1.3 us (3%)
  between operations  1.3 us (3%)
    pallas_call x1, Pallas kernels, body(): pl.pallas_call(functools.partial(step_kernel, n_slab, n_dom, far_scale),...  48.9 us
    mul x1, other arithmetic, body(): return (positions + 0.5 * time_increment * total, 0.5 * total)  1.3 us

profile of v2, /device:TPU:1, one launch (start us, length us, event | category | flops | bytes accessed | tf_op | source)
XLA Modules:
  0.0 51.5 jit_solution(17940257590989620017)
XLA Ops:
  1.3 0.0 copy-start
  1.3 48.9 %shard_map.77 = f32[3,512]{1,0:T(4,128)} custom-call(f32[3,512]{1,0:T(4,128)} %pos_ref.1, f32[3,512]{1,0:T(4,128)} %bur_ref.1, f32[1,512]{1,0:T(1,128)} %bitcast.2, s32[4]{0:T(128)} %cells_ref.1, s32[2,64]{1,0:T(2,128)} %bitcast.3, s32[1]{0:T(128)S(6)} %copy.8.count_ref), custom_call_target="tpu_custom_call" | custom-call | tf_op jit(solution)/shard_map/pallas_call | solution.py:452
  50.2 0.0 copy-done
  50.2 1.3 %broadcast_multiply_fusion = (f32[3,512]{1,0:T(4,128)}, f32[3,512]{1,0:T(4,128)}) fusion(f32[3,512]{1,0:T(4,128)} %shard_map.77, f32[3,512]{1,0:T(4,128)S(1)} %copy-done), kind=kLoop, calls=%fused_computation.1 | loop fusion | flops 4608 | bytes 24576 | tf_op jit(solution)/shard_map/mul | solution.py:486
Async XLA Ops:
  1.3 48.9 %copy-start = (f32[3,512]{1,0:T(4,128)S(1)}, f32[3,512]{1,0:T(4,128)}, u32[]{:S(2)}) copy-start(f32[3,512]{1,0:T(4,128)} %pos_ref.1) | copy-start | bytes 18436

commit v3 on v2

--- a/solution.py
+++ b/solution.py
@@ -16,8 +16,9 @@
 LANES = 128
 SLOTS = 64
 OWN = 16
-UNROLL = 8
-FIRST_PART = 24
+UNROLL = 16
+FIRST_PART = 48
+FAR_UNROLL = 8
 core_far = 9.0
 time_increment = 0.25
 around = [(ds, de) for ds in (-1, 0, 1) for de in (-1, 0, 1) if (ds, de) != (0, 0)]
@@ -78,10 +79,9 @@
     mom_y,
     mom_xc,
     mom_slab,
-    feats,
     bur_split,
-    q_buf,
     far_buf,
+    far_geo,
     pos_rows,
     mob_rows,
     send_sem,
@@ -89,7 +89,6 @@
 ):
     s = lax.axis_index("slab")
     e = lax.axis_index("dom")
-    halves = n_slab // 8
     row, lane = iotas()
     centre_x = (4 * s + 2).astype(F32)
     centre = jnp.where(row == 0, centre_x, jnp.where(row < 3, 4.0, 0.0))
@@ -142,9 +141,6 @@
         onehot[pl.ds(SLOTS + t, 1), :] = jnp.where(one_lane == to_b, 1.0, 0.0)
         return c
 
-    lax.fori_loop(0, SLOTS, place, 0)
-    onehot_t[...] = jnp.transpose(onehot[...])[:48].astype(BF16)
-
     bur_tiles = []
     for b in range(BLK):
         cols = slice(b * LANES, (b + 1) * LANES)
@@ -153,12 +149,20 @@
         for c in range(3):
             pos_rows[c, b : b + 1, :] = pos_ref[c : c + 1, cols]
         mob_rows[b : b + 1, :] = mob_ref[:, cols]
-        padded = jnp.concatenate([bur, jnp.zeros((5, LANES), F32)], axis=0)
-        bur_split[:, cols] = right_stack(split3(padded)).astype(BF16)
-    feats[...] = jnp.zeros(feats.shape, F32)
+
+    def set_up():
+        lax.fori_loop(0, SLOTS, place, 0)
+        onehot_t[...] = jnp.transpose(onehot[...])[:48].astype(BF16)
+        blank = jnp.zeros((3, LANES), F32)
+        for b, bur in enumerate(bur_tiles):
+            cols = slice(b * LANES, (b + 1) * LANES)
+            upper = jnp.concatenate([bur, blank, blank[0:2]], axis=0)
+            lower = jnp.concatenate([blank, bur, blank[0:2]], axis=0)
+            bur_split[0, :, cols] = right_stack(split3(upper)).astype(BF16)
+            bur_split[1, :, cols] = right_stack(split3(lower)).astype(BF16)
 
     def local_moments(phase):
-        sums = [jnp.zeros((8, LANES), F32) for _ in range(4)]
+        sums = [jnp.zeros((8, LANES), F32) for _ in range(6)]
         for b in range(BLK):
             tile = own[phase, b]
             inside = cells_ref[b] - 16 * s
@@ -168,17 +172,21 @@
             d1 = tile[1:2] - zy
             d2 = tile[2:3] - zz
             one = jnp.ones((1, LANES), F32)
-            mono = jnp.concatenate([one, d0, d1, d2, d0 * d0, d1 * d1, d2 * d2, d0 * d1], axis=0)
-            more = jnp.concatenate([d0 * d2, d1 * d2, jnp.zeros((6, LANES), F32)], axis=0)
+            squares = [3.0 * d * d for d in (d0, d1, d2)]
+            mono = jnp.concatenate([one, d0, d1, d2, *squares, 3.0 * d0 * d1], axis=0)
+            trace = -0.5 * (squares[0] + squares[1] + squares[2])
+            more = jnp.concatenate(
+                [3.0 * d0 * d2, 3.0 * d1 * d2, trace, jnp.zeros((5, LANES), F32)], axis=0
+            )
             spot = lane == 16 * row + inside
             for k in range(3):
                 bk = tile[3 + k : 4 + k]
                 m = jnp.sum(mono * bk, axis=1, keepdims=True)
                 sums[k] = sums[k] + jnp.where(spot, m, 0.0)
                 m = jnp.sum(more * bk, axis=1, keepdims=True)
-                sums[3] = sums[3] + jnp.where(lane == 16 * (row + 2 * k) + inside, m, 0.0)
-        rows = [jnp.sum(x, axis=0, keepdims=True) for x in sums]
-        mom_y[phase, y] = jnp.concatenate(rows, axis=0)
+                sums[3 + k] = sums[3 + k] + jnp.where(spot, m, 0.0)
+        rows = [jnp.sum(m, axis=0, keepdims=True) for m in sums]
+        mom_y[phase, y] = jnp.concatenate(rows + [jnp.zeros((2, LANES), F32)], axis=0)
 
     def remote(src, dst, phase, kind, target):
         return pltpu.make_async_remote_copy(
@@ -265,6 +273,25 @@
             return c
 
         lax.fori_loop(0, 9 * BLK // 2, two, 0)
+
+    def prepare_own(phase, p):
+        for c in range(3):
+            far_buf[c] = p[c]
+        for b in range(BLK):
+            tile = own[phase, b]
+            if phase == 0:
+                window[OWN + b] = tile
+        for half in range(2):
+            if phase == 1:
+                window_next[OWN // 2 + half] = own_next[half]
+        zz = (2 * (row % 4) + 1).astype(F32)
+        for t in range(BLK):
+            dz = p[2][t : t + 1] - zz
+            far_geo[2, t] = dz
+            for par in range(2):
+                dy = p[1][t : t + 1] - (2 * (2 * par + row // 4) + 1).astype(F32)
+                far_geo[par, t] = dy
+                far_geo[3 + par, t] = dy * dy + dz * dz + core_far
         for b in range(BLK):
             r = own[phase, b] - centre
             n = jnp.sum(jnp.where(row < 3, r * r, 0.0), axis=0, keepdims=True)
@@ -315,62 +342,46 @@
             for i in range(4):
                 give[phase, d, i] = acc[i][d * BLK : (d + 1) * BLK]
 
-    def swap_groups(m):
-        for d in (1, 2, 4):
-            up = pltpu.roll(pltpu.roll(m, 8 - d, 0), 16 * d, 1)
-            down = pltpu.roll(pltpu.roll(m, d, 0), LANES - 16 * d, 1)
-            rbit = (row // d) % 2
-            gbit = (lane // (16 * d)) % 2
-            m = jnp.where(rbit == gbit, m, jnp.where(rbit == 0, up, down))
-        return m
-
-    def far(phase, half):
-        for q in range(4):
-            rows = jnp.concatenate(
-                [mom_slab[phase, half * 8 + j, q : q + 1, :] for j in range(8)], axis=0
-            )
-            m = swap_groups(rows)
-            if q < 3:
-                for f in range(8):
-                    feats[f, q : q + 1, :] = m[f : f + 1] * (1.0 if f < 4 else 3.0)
-                feats[10, q : q + 1, :] = -1.5 * (m[4:5] + m[5:6] + m[6:7])
-            else:
-                for k in range(3):
-                    for f in (8, 9):
-                        j = 2 * k + f - 8
-                        feats[f, k : k + 1, :] = m[j : j + 1] * 3.0
-        for f in range(11):
-            stacked = left_stack(split3(feats[f])).astype(BF16)
-            q_buf[f] = mm(stacked, bur_split[...], 0, 0)
-
-        zz = (2 * (row % 4) + 1).astype(F32)
-
-        def group(g, acc):
-            acc = list(acc)
-            zx = (4 * (half * 8 + g // 2) + 2).astype(F32)
-            zy = (2 * (2 * (g % 2) + row // 4) + 1).astype(F32)
+    def far(phase):
+        def products(j):
+            stacked = jnp.transpose(left_stack(split3(mom_slab[phase, j]))).astype(BF16)
+            return mm(stacked, bur_split[0]), mm(stacked[0:48], bur_split[1])
+
+        def forces(j, found, acc):
+            q1, q2 = found
+            zx = (4 * j + 2).astype(F32)
             for t in range(BLK):
                 cols = slice(t * LANES, (t + 1) * LANES)
-                q = [q_buf[f, pl.ds(pl.multiple_of(8 * g, 8), 8), cols] for f in range(11)]
                 dx = jnp.broadcast_to(far_buf[0, t : t + 1, :] - zx, (8, LANES))
-                dy = far_buf[1, t : t + 1, :] - zy
-                dz = far_buf[2, t : t + 1, :] - zz
-                rs = lax.rsqrt(dx * dx + (dy * dy + dz * dz + core_far))
-                i2 = rs * rs
-                i3 = rs * i2
-                qr = q[1] * dx + q[2] * dy + q[3] * dz
-                tx = q[4] * dx + q[7] * dy + q[8] * dz
-                ty = q[7] * dx + q[5] * dy + q[9] * dz
-                tz = q[8] * dx + q[9] * dy + q[6] * dz
-                rqr = tx * dx + ty * dy + tz * dz
-                scal = q[0] + i2 * (3.0 * qr + q[10] + 2.5 * i2 * rqr)
-                acc[t] = acc[t] + i3 * (dx * scal - q[1] - i2 * tx)
-                acc[4 + t] = acc[4 + t] + i3 * (dy * scal - q[2] - i2 * ty)
-                acc[8 + t] = acc[8 + t] + i3 * (dz * scal - q[3] - i2 * tz)
+                dx2 = dx * dx
+                dz = far_geo[2, t]
+                for par in range(2):
+                    q = [q1[16 * f + 8 * par : 16 * f + 8 * par + 8, cols] for f in range(8)]
+                    q += [q2[16 * f + 8 * par : 16 * f + 8 * par + 8, cols] for f in range(3)]
+                    dy = far_geo[par, t]
+                    rs = lax.rsqrt(dx2 + far_geo[3 + par, t])
+                    i2 = rs * rs
+                    i3 = rs * i2
+                    tx = q[4] * dx + q[7] * dy + q[8] * dz
+                    ty = q[7] * dx + q[5] * dy + q[9] * dz
+                    tz = q[8] * dx + q[9] * dy + q[6] * dz
+                    qr = q[1] * dx + q[2] * dy + q[3] * dz
+                    rqr = tx * dx + ty * dy + tz * dz
+                    scal = q[0] + i2 * (3.0 * qr + q[10] + 2.5 * i2 * rqr)
+                    acc[t] = acc[t] + i3 * (dx * scal - q[1] - i2 * tx)
+                    acc[4 + t] = acc[4 + t] + i3 * (dy * scal - q[2] - i2 * ty)
+                    acc[8 + t] = acc[8 + t] + i3 * (dz * scal - q[3] - i2 * tz)
+            return acc
+
+        def turn(i, acc):
+            acc = list(acc)
+            for u in range(FAR_UNROLL):
+                j = FAR_UNROLL * i + u
+                acc = forces(j, products(j), acc)
             return tuple(acc)
 
         zero = jnp.zeros((8, LANES), F32)
-        return lax.fori_loop(0, 16, group, (zero,) * 12)
+        return lax.fori_loop(0, n_slab // FAR_UNROLL, turn, (zero,) * 12)
 
     def speed(phase):
         p = [far_buf[c] for c in range(3)]
@@ -383,10 +394,7 @@
         collect(phase)
         start_give(phase)
         all_of(phase, 3).wait_recv()
-        total = None
-        for half in range(halves):
-            acc = far(phase, half)
-            total = acc if total is None else [u + w for u, w in zip(total, acc)]
+        total = far(phase)
         all_of(phase, 4).wait_recv()
         got = [give[phase, 4, i] for i in range(4)]
         for d in range(9):
@@ -401,23 +409,16 @@
 
     def publish(phase, p):
         for b in range(BLK):
-            tile = jnp.concatenate(
+            own[phase, b] = jnp.concatenate(
                 [q[b : b + 1] for q in p] + [bur_tiles[b], jnp.zeros((2, LANES), F32)], axis=0
             )
-            own[phase, b] = tile
-            if phase == 0:
-                window[OWN + b] = tile
         if phase == 1:
             blank = jnp.zeros((1, LANES), F32)
             for half in range(2):
                 rows = []
                 for b in (2 * half, 2 * half + 1):
                     rows += [q[b : b + 1] for q in p] + [blank]
-                packed = jnp.concatenate(rows, axis=0)
-                own_next[half] = packed
-                window_next[OWN // 2 + half] = packed
-        for c in range(3):
-            far_buf[c] = p[c]
+                own_next[half] = jnp.concatenate(rows, axis=0)
         local_moments(phase)
 
     first_p = [pos_rows[c] for c in range(3)]
@@ -425,11 +426,14 @@
     pl.semaphore_wait(barrier, len(y_peers) + len(xc_peers) + len(z_peers) + len(around))
     start_y(0)
     start_halo(0)
+    set_up()
+    prepare_own(0, first_p)
     first_v = speed(0)
     second_p = [p + time_increment * v for p, v in zip(first_p, first_v)]
     publish(1, second_p)
     start_y(1)
     start_halo(1)
+    prepare_own(1, second_p)
     second_v = speed(1)
     for c in range(3):
         both = first_v[c] + second_v[c]
@@ -469,13 +473,12 @@
                 pltpu.VMEM((4, 2 * SLOTS, LANES), F32),
                 pltpu.VMEM((2, 9, 4, BLK, LANES), F32),
                 pltpu.VMEM((2, 9, 4, BLK, LANES), F32),
-                pltpu.VMEM((2, 8 if n_dom % 8 == 0 else n_dom, 4, LANES), F32),
-                pltpu.VMEM((2, 2 * (n_dom // 8 if n_dom % 8 == 0 else 1), 4, LANES), F32),
-                pltpu.VMEM((2, n_slab, 4, LANES), F32),
-                pltpu.VMEM((11, 8, LANES), F32),
-                pltpu.VMEM((48, segs), BF16),
-                pltpu.VMEM((11, LANES, segs), F32),
+                pltpu.VMEM((2, 8 if n_dom % 8 == 0 else n_dom, 8, LANES), F32),
+                pltpu.VMEM((2, 2 * (n_dom // 8 if n_dom % 8 == 0 else 1), 8, LANES), F32),
+                pltpu.VMEM((2, n_slab, 8, LANES), F32),
+                pltpu.VMEM((2, 48, segs), BF16),
                 pltpu.VMEM((3, BLK, LANES), F32),
+                pltpu.VMEM((5, BLK, 8, LANES), F32),
                 pltpu.VMEM((3, BLK, LANES), F32),
                 pltpu.VMEM((BLK, LANES), F32),
                 pltpu.SemaphoreType.DMA((2, 5)),

time: 51.7 us -> 49.4 us (0.956)
  Pallas kernels: 48.9 us -> 46.5 us
    pallas_call x1, Pallas kernels: 48.9 us -> 46.5 us  [body(): pl.pallas_call(functools.partial(step_kernel, n_slab, n_dom, far_scale),...]
where the time goes in v3:
time: 49.4 us; the launch traced here: 49.1 us
  Pallas kernels  46.5 us (94%)
  other arithmetic  1.3 us (3%)
  between operations  1.3 us (3%)
    pallas_call x1, Pallas kernels, body(): pl.pallas_call(functools.partial(step_kernel, n_slab, n_dom, far_scale),...  46.5 us
    mul x1, other arithmetic, body(): return (positions + 0.5 * time_increment * total, 0.5 * total)  1.3 us

profile of v3, /device:TPU:1, one launch (start us, length us, event | category | flops | bytes accessed | tf_op | source)
XLA Modules:
  0.0 49.1 jit_solution(16863173803743107852)
XLA Ops:
  1.3 0.0 copy-start
  1.3 46.5 %shard_map.77 = f32[3,512]{1,0:T(4,128)} custom-call(f32[3,512]{1,0:T(4,128)} %pos_ref.1, f32[3,512]{1,0:T(4,128)} %bur_ref.1, f32[1,512]{1,0:T(1,128)} %bitcast.2, s32[4]{0:T(128)} %cells_ref.1, s32[2,64]{1,0:T(2,128)} %bitcast.3, s32[1]{0:T(128)S(6)} %copy.8.count_ref), custom_call_target="tpu_custom_call" | custom-call | tf_op jit(solution)/shard_map/pallas_call | solution.py:456
  47.8 0.0 copy-done
  47.8 1.3 %broadcast_multiply_fusion = (f32[3,512]{1,0:T(4,128)}, f32[3,512]{1,0:T(4,128)}) fusion(f32[3,512]{1,0:T(4,128)} %shard_map.77, f32[3,512]{1,0:T(4,128)S(1)} %copy-done), kind=kLoop, calls=%fused_computation.1 | loop fusion | flops 4608 | bytes 24576 | tf_op jit(solution)/shard_map/mul | solution.py:489
Async XLA Ops:
  1.3 46.5 %copy-start = (f32[3,512]{1,0:T(4,128)S(1)}, f32[3,512]{1,0:T(4,128)}, u32[]{:S(2)}) copy-start(f32[3,512]{1,0:T(4,128)} %pos_ref.1) | copy-start | bytes 18436

commit v4 on v3

--- a/solution.py
+++ b/solution.py
@@ -18,10 +18,10 @@
 OWN = 16
 UNROLL = 16
 FIRST_PART = 48
-FAR_UNROLL = 8
+NEAR_Z = 2
 core_far = 9.0
 time_increment = 0.25
-around = [(ds, de) for ds in (-1, 0, 1) for de in (-1, 0, 1) if (ds, de) != (0, 0)]
+around = [(-1, -1), (-1, 1), (1, -1), (1, 1), (0, -1), (0, 1), (-1, 0), (1, 0)]
 
 
 def split3(x):
@@ -100,14 +100,15 @@
     nx = n_dom // ny
     nz = n_slab // 2
     x, y, z, core = e // ny, e % ny, s // 2, s % 2
-    y_peers = [(s, x * ny + lax.rem(y + i, ny)) for i in range(1, ny)]
+    far_first = lambda n: sorted(range(1, n), key=lambda i: -min(i, n - i))
+    y_peers = [(s, x * ny + lax.rem(y + i, ny)) for i in far_first(ny)]
     xc_peers = [
         (2 * z + lax.rem(core + c, 2), lax.rem(x + i, nx) * ny + y)
-        for i in range(nx)
+        for i in far_first(nx) + [0]
         for c in range(2)
         if (i, c) != (0, 0)
     ]
-    z_peers = [(2 * lax.rem(z + i, nz) + core, e) for i in range(1, nz)]
+    z_peers = [(2 * lax.rem(z + i, nz) + core, e) for i in far_first(nz)]
 
     barrier = pltpu.get_barrier_semaphore()
 
@@ -225,8 +226,8 @@
             parts = [mom_xc[phase, 2 * i + c] for i in range(nx)]
             mom_slab[phase, 2 * z + c] = sum(parts[1:], parts[0])
         mine = mom_slab.at[phase, pl.ds(2 * z, 2)]
-        for target in z_peers:
-            remote(mine, mine, phase, 3, target).start()
+        for i, target in zip(far_first(nz), z_peers):
+            remote(mine, mine, phase, 3 if min(i, nz - i) <= NEAR_Z else 5, target).start()
 
     def start_give(phase):
         for ds, de in around:
@@ -238,8 +239,9 @@
             window.at[pl.ds(0, 8 * BLK)] if phase == 0 else window_next.at[pl.ds(0, 16)],
             mom_y.at[phase, pl.ds(0, ny - 1)],
             mom_xc.at[phase, pl.ds(0, 2 * nx - 1)],
-            mom_slab.at[phase, pl.ds(0, 2 * (nz - 1))],
+            mom_slab.at[phase, pl.ds(0, 4 * NEAR_Z)],
             given.at[phase, pl.ds(0, 8)],
+            mom_slab.at[phase, pl.ds(0, 2 * (nz - 1) - 4 * NEAR_Z)],
         )[kind]
 
     def all_of(phase, kind):
@@ -342,7 +344,7 @@
             for i in range(4):
                 give[phase, d, i] = acc[i][d * BLK : (d + 1) * BLK]
 
-    def far(phase):
+    def far(phase, begin, end, acc):
         def products(j):
             stacked = jnp.transpose(left_stack(split3(mom_slab[phase, j]))).astype(BF16)
             return mm(stacked, bur_split[0]), mm(stacked[0:48], bur_split[1])
@@ -373,15 +375,11 @@
                     acc[8 + t] = acc[8 + t] + i3 * (dz * scal - q[3] - i2 * tz)
             return acc
 
-        def turn(i, acc):
-            acc = list(acc)
-            for u in range(FAR_UNROLL):
-                j = FAR_UNROLL * i + u
-                acc = forces(j, products(j), acc)
-            return tuple(acc)
-
-        zero = jnp.zeros((8, LANES), F32)
-        return lax.fori_loop(0, n_slab // FAR_UNROLL, turn, (zero,) * 12)
+        acc = list(acc)
+        for i in range(begin, end):
+            j = lax.rem(2 * (z + nz - NEAR_Z) + i, n_slab)
+            acc = forces(j, products(j), acc)
+        return acc
 
     def speed(phase):
         p = [far_buf[c] for c in range(3)]
@@ -393,8 +391,12 @@
         near(FIRST_PART, SLOTS)
         collect(phase)
         start_give(phase)
+        zero = jnp.zeros((8, LANES), F32)
+        middle = 4 * NEAR_Z + 2
         all_of(phase, 3).wait_recv()
-        total = far(phase)
+        total = far(phase, 0, middle, [zero] * 12)
+        all_of(phase, 5).wait_recv()
+        total = far(phase, middle, n_slab, total)
         all_of(phase, 4).wait_recv()
         got = [give[phase, 4, i] for i in range(4)]
         for d in range(9):
@@ -440,7 +442,7 @@
         for b in range(BLK):
             out_ref[c : c + 1, b * LANES : (b + 1) * LANES] = both[b : b + 1]
     for phase in range(2):
-        for kind in range(5):
+        for kind in range(6):
             all_of(phase, kind).wait_send()
 
 
@@ -481,8 +483,8 @@
                 pltpu.VMEM((5, BLK, 8, LANES), F32),
                 pltpu.VMEM((3, BLK, LANES), F32),
                 pltpu.VMEM((BLK, LANES), F32),
-                pltpu.SemaphoreType.DMA((2, 5)),
-                pltpu.SemaphoreType.DMA((2, 5)),
+                pltpu.SemaphoreType.DMA((2, 6)),
+                pltpu.SemaphoreType.DMA((2, 6)),
             ],
             compiler_params=pltpu.CompilerParams(collective_id=0, has_side_effects=True),
         )(positions, burgers, mobility.reshape(1, -1), block_cells, pairs.T, pair_count)

time: 49.4 us -> 48.3 us (0.978)
  Pallas kernels: 46.5 us -> 45.4 us
    pallas_call x1, Pallas kernels: 46.5 us -> 45.4 us  [body(): pl.pallas_call(functools.partial(step_kernel, n_slab, n_dom, far_scale),...]
where the time goes in v4:
time: 48.3 us; the launch traced here: 48 us
  Pallas kernels  45.4 us (94%)
  other arithmetic  1.3 us (3%)
  between operations  1.3 us (3%)
    pallas_call x1, Pallas kernels, body(): pl.pallas_call(functools.partial(step_kernel, n_slab, n_dom, far_scale),...  45.4 us
    mul x1, other arithmetic, body(): return (positions + 0.5 * time_increment * total, 0.5 * total)  1.3 us

profile of v4, /device:TPU:1, one launch (start us, length us, event | category | flops | bytes accessed | tf_op | source)
XLA Modules:
  0.0 48.0 jit_solution(4409257269117736676)
XLA Ops:
  1.3 0.0 copy-start
  1.3 45.4 %shard_map.77 = f32[3,512]{1,0:T(4,128)} custom-call(f32[3,512]{1,0:T(4,128)} %pos_ref.1, f32[3,512]{1,0:T(4,128)} %bur_ref.1, f32[1,512]{1,0:T(1,128)} %bitcast.2, s32[4]{0:T(128)} %cells_ref.1, s32[2,64]{1,0:T(2,128)} %bitcast.3, s32[1]{0:T(128)S(6)} %copy.8.count_ref), custom_call_target="tpu_custom_call" | custom-call | tf_op jit(solution)/shard_map/pallas_call | solution.py:458
  46.7 0.0 copy-done
  46.7 1.3 %broadcast_multiply_fusion = (f32[3,512]{1,0:T(4,128)}, f32[3,512]{1,0:T(4,128)}) fusion(f32[3,512]{1,0:T(4,128)} %shard_map.77, f32[3,512]{1,0:T(4,128)S(1)} %copy-done), kind=kLoop, calls=%fused_computation.1 | loop fusion | flops 4608 | bytes 24576 | tf_op jit(solution)/shard_map/mul | solution.py:491
Async XLA Ops:
  1.3 45.5 %copy-start = (f32[3,512]{1,0:T(4,128)S(1)}, f32[3,512]{1,0:T(4,128)}, u32[]{:S(2)}) copy-start(f32[3,512]{1,0:T(4,128)} %pos_ref.1) | copy-start | bytes 18436

commit v5 on v4

--- a/solution.py
+++ b/solution.py
@@ -274,7 +274,7 @@
             block(2 * i + 1, second)
             return c
 
-        lax.fori_loop(0, 9 * BLK // 2, two, 0)
+        lax.fori_loop(0, 9 * BLK // 2, two, 0, unroll=3)
 
     def prepare_own(phase, p):
         for c in range(3):

time: 48.3 us -> 48.1 us (level)
  no operation moved by 1% of the time
where the time goes in v5:
time: 48.1 us; the launch traced here: 47.9 us
  Pallas kernels  45.2 us (94%)
  other arithmetic  1.3 us (3%)
  between operations  1.3 us (3%)
    pallas_call x1, Pallas kernels, body(): pl.pallas_call(functools.partial(step_kernel, n_slab, n_dom, far_scale),...  45.2 us
    mul x1, other arithmetic, body(): return (positions + 0.5 * time_increment * total, 0.5 * total)  1.3 us

profile of v5, /device:TPU:1, one launch (start us, length us, event | category | flops | bytes accessed | tf_op | source)
XLA Modules:
  0.0 47.9 jit_solution(10095028435790839661)
XLA Ops:
  1.3 0.0 copy-start
  1.3 45.2 %shard_map.77 = f32[3,512]{1,0:T(4,128)} custom-call(f32[3,512]{1,0:T(4,128)} %pos_ref.1, f32[3,512]{1,0:T(4,128)} %bur_ref.1, f32[1,512]{1,0:T(1,128)} %bitcast.2, s32[4]{0:T(128)} %cells_ref.1, s32[2,64]{1,0:T(2,128)} %bitcast.3, s32[1]{0:T(128)S(6)} %copy.8.count_ref), custom_call_target="tpu_custom_call" | custom-call | tf_op jit(solution)/shard_map/pallas_call | solution.py:458
  46.5 0.0 copy-done
  46.6 1.3 %broadcast_multiply_fusion = (f32[3,512]{1,0:T(4,128)}, f32[3,512]{1,0:T(4,128)}) fusion(f32[3,512]{1,0:T(4,128)} %shard_map.77, f32[3,512]{1,0:T(4,128)S(1)} %copy-done), kind=kLoop, calls=%fused_computation.1 | loop fusion | flops 4608 | bytes 24576 | tf_op jit(solution)/shard_map/mul | solution.py:491
Async XLA Ops:
  1.3 45.3 %copy-start = (f32[3,512]{1,0:T(4,128)S(1)}, f32[3,512]{1,0:T(4,128)}, u32[]{:S(2)}) copy-start(f32[3,512]{1,0:T(4,128)} %pos_ref.1) | copy-start | bytes 18436
